TPU v7x, 256 devices: a whole 4x4x8 slice. The times are simulated.
256 devices in a mesh: ctx: 32 (over x, z), fsdp: 8 (over y, core).
Axes of the slice: x: 4, y: 4, z: 8, core: 2. Of those that a mesh axis runs over, the one named last changes fastest.
Arguments:
- query_in: bfloat16 [16384, 4096], P('ctx', 'fsdp'), may hold values from -6 to 6
- key_in: bfloat16 [16384, 4096], P('ctx', 'fsdp'), may hold values from -6 to 6
- value_in: bfloat16 [16384, 4096], P('ctx', 'fsdp'), may hold values from -6 to 6
- residues: float32 [16, 256], P(None, 'fsdp'), may hold values from -1.5 to 1.5
- decay_rate: float32 [16, 256], P(None, 'fsdp'), may hold values from 1.5258789e-05 to 0.1
- short_filter: float32 [3, 3, 4096], P(None, None, 'fsdp'), may hold values from -3 to 3
- skip_gain: float32 [1, 4096], P(None, 'fsdp'), may hold values from -3 to 3
Outputs:
- mixed_out: bfloat16 [16384, 4096], P('ctx', 'fsdp')
All inputs are finite; a program needn't handle non-finite values.
Results may differ from a plain program's by a relative error of at most 0.001.
Values may be sent and summed in bfloat16 or wider, within the bound.
A program may use at most 320 MiB of HBM per device.

v0:
```python
import jax
import jax.numpy as jnp
from jax import lax
from jax.sharding import PartitionSpec as P

SPAN = 512


def shifted(block, axis, distance):
    devices = range(lax.axis_size(axis))
    route = [(i - distance, i) for i in devices if i - distance in devices]
    return lax.ppermute(block, axis, route)


def in_order(parts, dim):
    parts = jnp.moveaxis(parts, 0, dim)
    lengths = parts.shape
    return parts.reshape(*lengths[:dim], lengths[dim] * lengths[dim + 1], *lengths[dim + 2 :])


def copy_for_each(shard, axis):
    length = lax.axis_size(axis)
    return lax.all_to_all(
        jnp.broadcast_to(shard[None], (length, *shard.shape)), axis, 0, 0, tiled=True
    )


def gather_directly(shard, axis, dim):
    return in_order(copy_for_each(shard, axis), dim)


def filter_taps(residues, decay_rate, count):
    norm = jnp.sqrt(-jnp.expm1(-2.0 * decay_rate))
    weight = residues * norm
    steps = jnp.arange(count).astype(jnp.float32)
    return jnp.sum(weight[:, :, None] * jnp.exp(-decay_rate[:, :, None] * steps), axis=0)


def toeplitz(taps):
    count = taps.shape[1]
    lag = jnp.arange(count)[:, None] - jnp.arange(count)[None, :]
    picked = jnp.take(taps, jnp.clip(lag, 0, count - 1), axis=1)
    return jnp.where(lag >= 0, picked, jnp.zeros_like(picked))


def short_conv(padded, weights, count):
    width = weights.shape[0]
    total = jnp.zeros((count, weights.shape[1]), jnp.float32)
    for shift_at in range(width):
        begin = width - 1 - shift_at
        total = total + weights[shift_at][None, :] * padded[begin : begin + count]
    return total


def body(query_in, key_in, value_in, residues, decay_rate, short_filter, skip_gain):
    local_len, width = query_in.shape
    modes, groups = residues.shape
    group_size = width // groups
    taps_len = short_filter.shape[1]
    block = SPAN
    count = local_len // block
    high = lax.Precision.HIGHEST
    edge = local_len - (taps_len - 1)
    rim = (query_in[edge:], key_in[edge:], value_in[edge:])
    prev_q, prev_k, prev_v = shifted((rim[0], rim[1], rim[2]), "ctx", 1)
    q_short = short_conv(
        jnp.concatenate([prev_q, query_in], 0).astype(jnp.float32), short_filter[0], local_len
    )
    k_short = short_conv(
        jnp.concatenate([prev_k, key_in], 0).astype(jnp.float32), short_filter[1], local_len
    )
    v_short = short_conv(
        jnp.concatenate([prev_v, value_in], 0).astype(jnp.float32), short_filter[2], local_len
    )
    gated = k_short * v_short
    blocks = gated.reshape(count, block, groups, group_size)
    toe = toeplitz(filter_taps(residues, decay_rate, block))
    local = jnp.einsum("gts,ksgj->ktgj", toe, blocks, precision=high)
    norm = jnp.sqrt(-jnp.expm1(-2.0 * decay_rate))
    weight = residues * norm
    steps = jnp.arange(block).astype(jnp.float32)
    lead = weight[:, :, None] * jnp.exp(-decay_rate[:, :, None] * (steps + 1.0))
    tail = jnp.exp(-decay_rate[:, :, None] * (block - 1.0 - steps))
    block_fresh = jnp.einsum("ngs,ksgj->kngj", tail, blocks, precision=high)
    block_power = jnp.exp(-decay_rate * block)

    def carry_step(state, item):
        return (state * block_power[:, :, None] + item, state)

    own_final, own_prefix = lax.scan(
        carry_step, jnp.zeros((modes, groups, group_size), jnp.float32), block_fresh
    )
    fresh = own_final.reshape(modes, width)
    me_index = lax.axis_index("ctx")
    piece = gather_directly(fresh, "ctx", 0)
    owners_count = piece.shape[0] // modes
    pieces = piece.reshape(owners_count, modes, width)
    owner = jnp.arange(owners_count)
    gap = me_index - 1 - owner
    gap_f = jnp.maximum(gap, 0).astype(jnp.float32)
    factor = jnp.exp(-decay_rate[None] * (local_len * gap_f[:, None, None]))
    factor = jnp.where(gap[:, None, None] >= 0, factor, jnp.zeros_like(factor))
    spread = jnp.repeat(factor, group_size, axis=2)
    state_in = jnp.sum(spread * pieces, axis=0)
    block_steps = jnp.arange(count).astype(jnp.float32)
    reach = jnp.exp(-decay_rate[None] * (block * block_steps[:, None, None]))
    entering = own_prefix + state_in.reshape(modes, groups, group_size)[None] * reach[..., None]
    term = jnp.einsum("ngt,kngj->ktgj", lead, entering, precision=high)
    long_conv = (local + term).reshape(local_len, width)
    return (q_short * (long_conv + skip_gain[0][None, :] * gated)).astype(jnp.bfloat16)


def solution(mesh):
    placed = (
        P("ctx", "fsdp"),
        P("ctx", "fsdp"),
        P("ctx", "fsdp"),
        P(None, "fsdp"),
        P(None, "fsdp"),
        P(None, None, "fsdp"),
        P(None, "fsdp"),
    )
    return jax.shard_map(
        body, mesh=mesh, in_specs=placed, out_specs=P("ctx", "fsdp"), check_vma=False
    )
```

profile of v0, /device:TPU:6, one launch (start us, length us, event | category | flops | bytes accessed | tf_op | source)
XLA Modules:
  0.0 1033.7 jit_solution(827099555869974571)
XLA Ops:
  0.0 0.0 copy-start.1
  0.0 0.0 copy-start.2
  0.0 0.8 slice.92
  0.8 0.2 copy.48
  1.0 3.8 collective-permute-start.1
  4.8 0.7 slice.99
  5.5 0.2 copy.50
  5.7 3.8 collective-permute-start.2
  9.5 0.7 slice.85
  10.3 0.2 copy.46
  10.4 3.8 collective-permute-start
  14.3 0.1 fusion.9
  14.5 1.1 fusion.25
  15.5 1.5 fusion.40
  17.0 1.3 multiply_exponential_fusion
  18.3 0.1 copy.53
  18.4 0.1 copy.52
  18.5 0.3 copy.61
  18.7 0.1 broadcast_clamp_fusion
  18.9 0.8 exponential_select_fusion
  19.7 0.4 multiply_reduce_fusion
  20.1 0.0 copy-done.1
  20.1 0.2 copy.49
  20.3 0.0 copy-done.2
  20.3 0.2 copy.51
  20.6 0.1 copy.56
  20.6 0.0 collective-permute-done.1
  20.6 0.3 maximum_convert_fusion.1
  21.0 0.0 copy-done.4
  21.0 0.0 collective-permute-done.2
  21.0 0.3 maximum_convert_fusion.2
  21.3 2.6 fusion.11
  23.9 0.0 copy-start.3
  23.9 1.5 fusion.22
  25.5 0.1 copy.57
  25.6 1.1 broadcast_in_dim.68
  26.7 8.8 all-to-all-start
  35.5 0.6 fusion.35
  36.1 0.0 copy-done.3
  36.1 1.0 copy.47
  37.1 0.1 copy.54
  37.3 865.8 %gather_fusion = f32[262144,32]{1,0:T(8,128)} fusion(f32[32,512]{0,1:T(8,128)S(1)} %copy.54, s32[262144]{0:T(1024)S(1)} %broadcast_clamp_fusion), kind=kCustom, calls=%fused_computation | custom fusion | bytes 68157440 | tf_op jit(solution)/shard_map/jit(_take)/gather | solution.py:42
  903.1 85.7 %copy.55 = f32[512,512,32]{1,0,2:T(8,128)} copy(f32[512,512,32]{2,1,0:T(8,128)} %bitcast.10) | data formatting | bytes 67108864 | tf_op jit(solution)/shard_map/jit(_take)/gather | solution.py:42
  988.8 0.0 collective-permute-done
  988.8 0.0 copy-done
  988.8 0.3 maximum_convert_fusion
  989.1 32.2 %fusion = f32[32,16,512]{2,1,0:T(8,128)S(1)} fusion(f32[512,32,16]{0,2,1:T(8,128)S(1)} %bitcast.42, f32[512,512,32]{1,0,2:T(8,128)} %copy.55, pred[512,512]{1,0:T(8,128)(4,1)} %get-tuple-element.33, pred[512,512]{1,0:T(8,128)(4,1)} %get-tuple-element.34), kind=kOutput, calls=%fused_computation.1 | convolution fusion | flops 1627389952 | bytes 36175872 | tf_op jit(solution)/shard_map/gts,ksgj->ktgj/dot_general | solution.py:78
  1021.4 0.0 copy-start.5
  1021.4 0.0 copy-start.10
  1021.4 0.0 all-to-all-done
  1021.4 3.6 copy.58
  1025.0 3.4 fusion.8
  1028.4 0.8 broadcast_in_dim_reshape.4
  1029.2 0.0 copy-done.6
  1029.2 1.1 broadcast_multiply_fusion
  1030.3 0.0 copy-done.5
  1030.3 0.0 copy-done.10
  1030.3 1.3 convolution_add_fusion
  1031.7 0.0 copy-done.7
  1031.7 0.0 copy-done.8
  1031.7 0.0 copy-done.9
  1031.7 0.0 copy-done.11
  1031.7 1.0 fusion.17
  1032.7 1.0 copy.60
  (12 shorter events, 0.1 us)
Async XLA Ops:
  0.0 20.1 %copy-start.1 = (bf16[512,512]{1,0:T(8,128)(2,1)S(1)}, bf16[512,512]{1,0:T(8,128)(2,1)}, u32[]{:S(2)}) copy-start(bf16[512,512]{1,0:T(8,128)(2,1)} %param.8) | copy-start | bytes 1572868
  0.0 20.3 %copy-start.2 = (bf16[512,512]{1,0:T(8,128)(2,1)S(1)}, bf16[512,512]{1,0:T(8,128)(2,1)}, u32[]{:S(2)}) copy-start(bf16[512,512]{1,0:T(8,128)(2,1)} %param.9) | copy-start | bytes 1572868
  1.0 19.7 %collective-permute-start.1 = (bf16[2,512]{0,1:T(8,128)(2,1)S(1)}, bf16[2,512]{0,1:T(8,128)(2,1)S(1)}, u32[]{:S(2)}, u32[]{:S(2)}) collective-permute-start(bf16[2,512]{0,1:T(8,128)(2,1)S(1)} %copy.48), channel_id=1, source_target_pairs={{0,8},{8,16},{16,24},{24,32},{32,40},{40,48},{48,56},{56,64},{64,7... | collective-permute-start | bytes 6152 | tf_op jit(solution)/shard_map/ppermute | solution.py:12
  5.7 15.3 %collective-permute-start.2 = (bf16[2,512]{0,1:T(8,128)(2,1)S(1)}, bf16[2,512]{0,1:T(8,128)(2,1)S(1)}, u32[]{:S(2)}, u32[]{:S(2)}) collective-permute-start(bf16[2,512]{0,1:T(8,128)(2,1)S(1)} %copy.50), channel_id=1, source_target_pairs={{0,8},{8,16},{16,24},{24,32},{32,40},{40,48},{48,56},{56,64},{64,7... | collective-permute-start | bytes 6152 | tf_op jit(solution)/shard_map/ppermute | solution.py:12
  10.4 978.3 %collective-permute-start = (bf16[2,512]{0,1:T(8,128)(2,1)S(1)}, bf16[2,512]{0,1:T(8,128)(2,1)S(1)}, u32[]{:S(2)}, u32[]{:S(2)}) collective-permute-start(bf16[2,512]{0,1:T(8,128)(2,1)S(1)} %copy.46), channel_id=1, source_target_pairs={{0,8},{8,16},{16,24},{24,32},{32,40},{40,48},{48,56},{56,64},{64,7... | collective-permute-start | bytes 6152 | tf_op jit(solution)/shard_map/ppermute | solution.py:12
  18.5 2.5 copy-start.4
  23.9 12.2 %copy-start.3 = (bf16[512,512]{1,0:T(8,128)(2,1)S(1)}, bf16[512,512]{1,0:T(8,128)(2,1)}, u32[]{:S(2)}) copy-start(bf16[512,512]{1,0:T(8,128)(2,1)} %param.7) | copy-start | bytes 1572868
  26.7 994.7 %all-to-all-start = ((f32[32,16,512]{2,1,0:T(8,128)}), f32[32,16,512]{2,1,0:T(8,128)}, u32[]{:S(2)}, u32[]{:S(2)}) async-start(f32[32,16,512]{2,1,0:T(8,128)} %broadcast_in_dim.68), calls=%async_computation | async-start | bytes 2097152 | tf_op jit(solution)/shard_map/all_to_all | solution.py:23
  903.0 85.7 %copy-start = (bf16[512,512]{0,1:T(8,128)(2,1)S(1)}, bf16[512,512]{0,1:T(8,128)(2,1)}, u32[]{:S(2)}) copy-start(bf16[512,512]{0,1:T(8,128)(2,1)} %copy.47) | copy-start | bytes 1572868
  1021.3 7.9 copy-start.6
  1021.4 9.0 copy-start.5
  1021.4 9.0 copy-start.10
  1025.0 6.7 copy-start.7
  1025.0 6.7 copy-start.8
  1025.0 6.7 copy-start.9
  1025.0 6.7 copy-start.11
where the time goes:
time: 1040 us; the launch traced here: 1030 us
  local copies, waits for them, and re-layouts  965 us (93%)
  matrix products  35.1 us (3%)
  starting transfers between devices  20.3 us (2%)
  other arithmetic  13.5 us (1%)
    gather x2, local copies, waits for them, and re-layouts, toeplitz(): picked = jnp.take(taps, jnp.clip(lag, 0, count - 1), axis=1)  952 us
    dot_general x1, matrix products, body(): local = jnp.einsum('gts,ksgj->ktgj', toe, blocks, precision=high)  32.2 us
  transfers between devices with their start and end apart: 4, of which 0 were waited for; matrix products, arithmetic and copies ran while one was open for 97% of the time, Pallas kernels for 0%

commit v1 on v0

v1 whole, which is shorter than its diff:
```python
import functools

import jax
import jax.numpy as jnp
from jax import lax
from jax.experimental import pallas as pl
from jax.experimental.pallas import tpu as pltpu
from jax.sharding import PartitionSpec as P

MESH = pl.DeviceIdType.MESH
NX, NZ = 4, 8
SEGS = 8
LANES = 128
FRONT = 8


def to_device(src, dst, send, recv, ctx):
    return pltpu.make_async_remote_copy(
        src_ref=src,
        dst_ref=dst,
        send_sem=send,
        recv_sem=recv,
        device_id={"ctx": ctx},
        device_id_type=MESH,
    )


def one_minus_exp(u):
    series = u * (1 - u / 2 * (1 - u / 3 * (1 - u / 4 * (1 - u / 5 * (1 - u / 6 * (1 - u / 7))))))
    return jnp.where(u < 0.3, series, 1 - jnp.exp(-u))


def scan_segments(value, powers, row):
    for power, step in zip(powers, (1, 2, 4)):
        value = value + power * jnp.where(row >= step, pltpu.roll(value, step, 0), 0.0)
    return value


def split(x):
    high = x.astype(jnp.bfloat16)
    return high, (x - high.astype(jnp.float32)).astype(jnp.bfloat16)


def kernel(
    query, key, value, residues, decay_rate, short_filter, skip_gain,
    out,
    raw, wide, params_r, params_d, filt, skip,
    decay, weight, gated, final, base, qs, lead_hi, lead_lo,
    fresh, lines, edge, rim, delta_own, delta, total, totals, own_sum, far_sum,
    in_sem, line_send, line_recv, delta_send, delta_recv, total_send, total_recv, rim_send, rim_recv,
):
    rows, width = query.shape
    modes, groups = residues.shape
    size = width // groups
    steps = rows // SEGS
    tiles = width // LANES
    f32 = jnp.float32

    me = lax.axis_index("ctx")
    x, z = me // NZ, lax.rem(me, NZ)

    def line_peer(k):
        return x * NZ + lax.rem(z + k, NZ)

    barrier = pltpu.get_barrier_semaphore()

    def here(ctx):
        pl.semaphore_signal(barrier, inc=1, device_id={"ctx": ctx}, device_id_type=MESH)

    for k in range(1, NZ):
        here(line_peer(k))
    for k in range(1, NX):
        pl.when(x >= k)(functools.partial(here, me - k * NZ))
    pl.when((z == 0) & (x > 0))(functools.partial(here, me - 1))

    small = [
        pltpu.make_async_copy(a, b, in_sem.at[i])
        for i, (a, b) in enumerate(
            ((residues, params_r), (decay_rate, params_d), (short_filter, filt), (skip_gain, skip))
        )
    ]
    large = [
        pltpu.make_async_copy(a, raw.at[p], in_sem.at[4 + p])
        for p, a in enumerate((query, key, value))
    ]
    for copy in (small[1], small[0], small[2], large[1], large[2], large[0], small[3]):
        copy.start()

    small[0].wait()
    small[1].wait()
    small[2].wait()
    lane = lax.broadcasted_iota(jnp.int32, (groups, width), 1)
    group = lax.broadcasted_iota(jnp.int32, (groups, width), 0)
    pick = (lane // size == group).astype(f32)
    high = lax.Precision.HIGHEST
    rate = jnp.dot(params_d[...], pick, precision=high, preferred_element_type=f32)
    decay[...] = rate
    residue = jnp.dot(params_r[...], pick, precision=high, preferred_element_type=f32)
    weight[...] = residue * jnp.sqrt(one_minus_exp(2.0 * rate))

    row = lax.broadcasted_iota(jnp.int32, (SEGS, LANES), 0)

    def widen(p):
        for t in range(tiles):
            wide[p, t, 0:FRONT] = jnp.zeros((FRONT, LANES), f32)
            wide[p, t, FRONT:] = raw[p, :, t * LANES : (t + 1) * LANES].astype(f32)

    large[1].wait()
    widen(1)
    large[2].wait()
    widen(2)

    def segments(p, offset, tile):
        return wide[p, tile, pl.ds(FRONT + offset, SEGS, stride=steps)]

    def taps_of(p, cols):
        return [jnp.broadcast_to(filt[p, i : i + 1, cols], (SEGS, LANES)) for i in range(3)]

    def short(taps, now, last, older):
        return taps[0] * now + taps[1] * last + taps[2] * older

    for tile in range(tiles):
        cols = slice(tile * LANES, (tile + 1) * LANES)
        ktaps, vtaps = taps_of(1, cols), taps_of(2, cols)
        rates = [
            jnp.broadcast_to(jnp.exp(-decay[n : n + 1, cols]), (SEGS, LANES)) for n in range(modes)
        ]

        def advance(j, carry, tile=tile, cols=cols, ktaps=ktaps, vtaps=vtaps, rates=rates):
            k1, k2, v1, v2, states = carry
            k0, v0 = segments(1, j, tile), segments(2, j, tile)
            g = short(ktaps, k0, k1, k2) * short(vtaps, v0, v1, v2)
            gated[pl.ds(pl.multiple_of(j * SEGS, SEGS), SEGS), cols] = g
            states = tuple(s * a + g for s, a in zip(states, rates))
            return k0, k1, v0, v1, states

        zero = jnp.zeros((SEGS, LANES), f32)
        first = (
            segments(1, -1, tile), segments(1, -2, tile),
            segments(2, -1, tile), segments(2, -2, tile),
            (zero,) * modes,
        )
        states = lax.fori_loop(0, steps, advance, first, unroll=4)[4]
        for n in range(modes):
            final[n, :, cols] = states[n]
            powers = [jnp.exp(-decay[n : n + 1, cols] * (steps * s)) for s in (1, 2, 4)]
            fresh[n : n + 1, cols] = scan_segments(states[n], powers, row)[SEGS - 1 : SEGS]

    large[0].wait()
    for p in range(3):
        edge[2 * p : 2 * p + 2] = raw[p, rows - 8 : rows].astype(f32)[6:8]
    pl.semaphore_wait(
        barrier, NZ - 1 + NX - 1 - x + jnp.where((z == NZ - 1) & (x < NX - 1), 1, 0)
    )
    last = NX * NZ - 1
    rim_copy = to_device(edge, rim, rim_send, rim_recv, me + 1)
    pl.when(me < last)(rim_copy.start)
    line_copies = {
        k: to_device(fresh, lines.at[z], line_send.at[k], line_recv.at[k], line_peer(k))
        for k in range(1, NZ)
    }
    for k in (4, 3, 5, 2, 6, 1, 7):
        line_copies[k].start()
    lines[z] = fresh[...]

    lane = lax.broadcasted_iota(jnp.int32, (modes, width), 1)
    mode = lax.broadcasted_iota(jnp.int32, (modes, width), 0)
    own = lax.rem(lane, modes) == mode
    flat_rate = jnp.sum(jnp.where(own, decay[...], 0.0), axis=0, keepdims=True)
    flat_weight = jnp.sum(jnp.where(own, weight[...], 0.0), axis=0, keepdims=True)
    for tile in range(tiles):
        cols = slice(tile * LANES, (tile + 1) * LANES)
        rate8 = jnp.broadcast_to(flat_rate[:, cols], (16, LANES))
        row16 = lax.broadcasted_iota(jnp.int32, (16, LANES), 0).astype(f32)
        begin = flat_weight[:, cols] * jnp.exp(-rate8 * (row16 + 1.0))
        jump = jnp.exp(-rate8 * 16.0)

        def lead_rows(i, now, cols=cols, jump=jump):
            at = pl.ds(pl.multiple_of(i * 16, 16), 16)
            hi, lo = split(now)
            lead_hi[at, cols] = hi
            lead_lo[at, cols] = lo
            return now * jump

        lax.fori_loop(0, rows // 16, lead_rows, begin, unroll=4)
    widen(0)
    small[3].wait()

    @pl.when(me == 0)
    def _():
        rim[...] = jnp.zeros_like(rim)

    pl.when(me > 0)(rim_copy.wait_recv)
    for tile in range(tiles):
        cols = slice(tile * LANES, (tile + 1) * LANES)
        for p in range(3):
            wide[p, tile, FRONT - 2 : FRONT] = rim[2 * p : 2 * p + 2, cols]

        def head(p, tile=tile, cols=cols):
            front = wide[p, tile, FRONT - 2 : FRONT + 2]
            return sum(filt[p, i : i + 1, cols] * front[2 - i : 4 - i] for i in range(3))

        true_head = head(1) * head(2)
        for i in range(2):
            at = slice(i * SEGS, i * SEGS + 1)
            delta_own[i : i + 1, cols] = true_head[i : i + 1] - gated[at, cols]
            gated[at, cols] = true_head[i : i + 1]
    delta_copies = {
        k: to_device(delta_own, delta.at[z], delta_send.at[k], delta_recv.at[k], line_peer(k))
        for k in range(1, NZ)
    }
    for k in (4, 3, 5, 2, 6, 1, 7):
        delta_copies[k].start()
    delta[z] = delta_own[...]

    for tile in range(tiles):
        cols = slice(tile * LANES, (tile + 1) * LANES)
        qtaps = taps_of(0, cols)
        gain = jnp.broadcast_to(skip[0:1, cols], (SEGS, LANES))
        d0, d1 = delta_own[0:1, cols], delta_own[1:2, cols]
        rates, weights, entering = [], [], []
        for n in range(modes):
            rate = decay[n : n + 1, cols]
            powers = [jnp.exp(-rate * (steps * s)) for s in (1, 2, 4)]
            extra = jnp.exp(-rate * (steps - 1.0)) * d0 + jnp.exp(-rate * (steps - 2.0)) * d1
            state = final[n, :, cols] + jnp.where(row == 0, extra, 0.0)
            state = scan_segments(state, powers, row)
            entering.append(jnp.where(row >= 1, pltpu.roll(state, 1, 0), 0.0))
            rates.append(jnp.broadcast_to(jnp.exp(-rate), (SEGS, LANES)))
            weights.append(jnp.broadcast_to(weight[n : n + 1, cols], (SEGS, LANES)))

        def respond(j, carry, tile=tile, cols=cols, qtaps=qtaps, gain=gain, rates=rates, weights=weights):
            q1, q2, states = carry
            q0 = segments(0, j, tile)
            g = gated[pl.ds(pl.multiple_of(j * SEGS, SEGS), SEGS), cols]
            states = tuple(s * a + g for s, a in zip(states, rates))
            terms = [s * w for s, w in zip(states, weights)] + [gain * g]
            while len(terms) > 1:
                terms = [sum(terms[i : i + 2]) for i in range(0, len(terms), 2)]
            q = short(qtaps, q0, q1, q2)
            at = pl.ds(j, SEGS, stride=steps)
            base[tile, at] = q * terms[0]
            qs[tile, at] = q
            return q0, q1, states

        first = (segments(0, -1, tile), segments(0, -2, tile), tuple(entering))
        lax.fori_loop(0, steps, respond, first, unroll=4)

    block = jnp.exp(-decay[...] * rows)
    late0 = jnp.exp(-decay[...] * (rows - 1.0))
    late1 = jnp.exp(-decay[...] * (rows - 2.0))
    hop = jnp.exp(-decay[...] * (rows * NZ))
    for k in range(1, NZ):
        line_copies[k].wait_recv()
        delta_copies[k].wait_recv()
    carried = jnp.zeros((modes, width), f32)
    prefix = carried
    for i in range(NZ):
        prefix = jnp.where(z == i, carried, prefix)
        carried = carried * block + lines[i] + late0 * delta[i, 0:1] + late1 * delta[i, 1:2]
    total[...] = carried
    own_sum[...] = prefix
    total_copies = {
        k: to_device(total, totals.at[x], total_send.at[k], total_recv.at[k], me + k * NZ)
        for k in range(1, NX)
    }
    for k in range(1, NX):
        pl.when(x + k < NX)(total_copies[k].start)

    far_sum[...] = jnp.zeros((modes, width), f32)
    for i in range(NX - 1):

        @pl.when(x > i)
        def _(i=i):
            to_device(total, totals.at[i], total_send.at[0], total_recv.at[x - i], me).wait_recv()
            far_sum[...] = far_sum[...] * hop + totals[i]

    state = own_sum[...] + jnp.exp(-decay[...] * (rows * z.astype(f32))) * far_sum[...]

    span = 256
    grow = lax.broadcasted_iota(jnp.int32, (span, span), 0) // modes
    gcol = lax.broadcasted_iota(jnp.int32, (span, span), 1) // size
    for u in range(width // span):
        cols = slice(u * span, (u + 1) * span)
        part = state[:, cols]
        blocks = jnp.where(grow == gcol, jnp.concatenate([part] * (span // modes), axis=0), 0.0)
        hi, lo = split(blocks)
        lh, ll = lead_hi[:, cols], lead_lo[:, cols]
        add = jnp.dot(lh, hi, preferred_element_type=f32)
        add += jnp.dot(lh, lo, preferred_element_type=f32)
        add += jnp.dot(ll, hi, preferred_element_type=f32)
        for i in range(span // LANES):
            t = u * (span // LANES) + i
            part = add[:, i * LANES : (i + 1) * LANES]
            out[:, t * LANES : (t + 1) * LANES] = (base[t] + qs[t] * part).astype(jnp.bfloat16)

    pl.when(me < last)(rim_copy.wait_send)
    for k in range(1, NZ):
        line_copies[k].wait_send()
        delta_copies[k].wait_send()
    for k in range(1, NX):
        pl.when(x + k < NX)(total_copies[k].wait_send)


def body(query_in, key_in, value_in, residues, decay_rate, short_filter, skip_gain):
    rows, width = query_in.shape
    modes = residues.shape[0]
    f32 = jnp.float32
    vmem = lambda *shape, dtype=f32: pltpu.VMEM(shape, dtype)
    dma = pltpu.SemaphoreType.DMA
    anywhere = pl.BlockSpec(memory_space=pl.ANY)
    return pl.pallas_call(
        kernel,
        out_shape=jax.ShapeDtypeStruct((rows, width), jnp.bfloat16),
        in_specs=[anywhere] * 7,
        out_specs=pl.BlockSpec(memory_space=pltpu.VMEM),
        scratch_shapes=[
            vmem(3, rows, width, dtype=jnp.bfloat16),
            vmem(3, width // LANES, FRONT + rows, LANES),
            vmem(*residues.shape),
            vmem(*decay_rate.shape),
            vmem(*short_filter.shape),
            vmem(*skip_gain.shape),
            vmem(modes, width),
            vmem(modes, width),
            vmem(rows, width),
            vmem(modes, SEGS, width),
            vmem(width // LANES, rows, LANES),
            vmem(width // LANES, rows, LANES),
            vmem(rows, width, dtype=jnp.bfloat16),
            vmem(rows, width, dtype=jnp.bfloat16),
            vmem(modes, width),
            vmem(NZ, modes, width),
            vmem(8, width),
            vmem(8, width),
            vmem(2, width),
            vmem(NZ, 2, width),
            vmem(modes, width),
            vmem(NX, modes, width),
            vmem(modes, width),
            vmem(modes, width),
            dma((7,)),
            dma((NZ,)), dma((NZ,)),
            dma((NZ,)), dma((NZ,)),
            dma((NX,)), dma((NX,)),
            dma, dma,
        ],
        compiler_params=pltpu.CompilerParams(
            collective_id=0, has_side_effects=True, vmem_limit_bytes=40 * 2**20
        ),
    )(query_in, key_in, value_in, residues, decay_rate, short_filter, skip_gain)


def solution(mesh):
    placed = (
        P("ctx", "fsdp"),
        P("ctx", "fsdp"),
        P("ctx", "fsdp"),
        P(None, "fsdp"),
        P(None, "fsdp"),
        P(None, None, "fsdp"),
        P(None, "fsdp"),
    )
    return jax.shard_map(
        body, mesh=mesh, in_specs=placed, out_specs=P("ctx", "fsdp"), check_vma=False
    )
```

time: 1040 us -> 29.3 us (0.03)
  local copies, waits for them, and re-layouts: 965 us -> 6.73 us
  matrix products: 35.1 us -> 0 us
  Pallas kernels: 0 us -> 22.2 us
  starting transfers between devices: 20.3 us -> 0 us
  other arithmetic: 13.5 us -> 0 us
    gather x2 -> x0, local copies, waits for them, and re-layouts: 952 us -> none  [toeplitz(): picked = jnp.take(taps, jnp.clip(lag, 0, count - 1), axis=1)]
    dot_general x3 -> x0, matrix products: 35.1 us -> none  [the longest x1 32.2 us: body(): local = jnp.einsum('gts,ksgj->ktgj', toe, blocks, precision=high)]
    pallas_call x0 -> x1, Pallas kernels: none -> 22.2 us  [body(): pl.pallas_call(kernel, out_shape=jax.ShapeDtypeStruct((rows, width), jnp....]
    ppermute x3 -> x0, starting transfers between devices: 11.5 us -> none  [shifted(): return lax.ppermute(block, axis, route)]
  transfers between devices with their start and end apart: 4 -> 0, of which waited for: 0 -> 0; matrix products, arithmetic and copies ran while one was open for 97% -> 0% of each run, Pallas kernels for 0% -> 0%
where the time goes in v1:
time: 29.3 us; the launch traced here: 28.9 us
  Pallas kernels  22.2 us (76%)
  local copies, waits for them, and re-layouts  6.73 us (23%)
    pallas_call x1, Pallas kernels, body(): pl.pallas_call(kernel, out_shape=jax.ShapeDtypeStruct((rows, width), jnp....  22.2 us
    unnamed x15, local copies, waits for them, and re-layouts  6.73 us

profile of v1, /device:TPU:6, one launch (start us, length us, event | category | flops | bytes accessed | tf_op | source)
XLA Modules:
  0.0 28.9 jit_solution(10961437754207068477)
XLA Ops:
  0.0 0.0 copy-start
  0.0 1.0 %copy-done = bf16[512,512]{1,0:T(8,128)(2,1)S(1)} copy-done((bf16[512,512]{1,0:T(8,128)(2,1)S(1)}, bf16[512,512]{1,0:T(8,128)(2,1)}, u32[]{:S(2)}) %copy-start) | copy-done | bytes 524312
  1.0 0.0 copy-start.1
  1.0 1.0 %copy-done.1 = bf16[512,512]{1,0:T(8,128)(2,1)S(1)} copy-done((bf16[512,512]{1,0:T(8,128)(2,1)S(1)}, bf16[512,512]{1,0:T(8,128)(2,1)}, u32[]{:S(2)}) %copy-start.1) | copy-done | bytes 524312
  2.1 0.0 copy-start.2
  2.1 1.0 %copy-done.2 = bf16[512,512]{1,0:T(8,128)(2,1)S(1)} copy-done((bf16[512,512]{1,0:T(8,128)(2,1)S(1)}, bf16[512,512]{1,0:T(8,128)(2,1)}, u32[]{:S(2)}) %copy-start.2) | copy-done | bytes 524312
  3.1 0.0 copy-start.3
  3.1 0.7 %copy-done.3 = f32[3,3,512]{2,1,0:T(4,128)S(1)} copy-done((f32[3,3,512]{2,1,0:T(4,128)S(1)}, f32[3,3,512]{2,1,0:T(4,128)}, u32[]{:S(2)}) %copy-start.3) | copy-done | bytes 18456
  3.9 0.0 copy-start.4
  3.9 0.7 %copy-done.4 = f32[16,32]{1,0:T(8,128)S(1)} copy-done((f32[16,32]{1,0:T(8,128)S(1)}, f32[16,32]{1,0:T(8,128)}, u32[]{:S(2)}) %copy-start.4) | copy-done | bytes 2072
  4.6 0.0 copy-start.5
  4.6 0.7 %copy-done.5 = f32[16,32]{1,0:T(8,128)S(1)} copy-done((f32[16,32]{1,0:T(8,128)S(1)}, f32[16,32]{1,0:T(8,128)}, u32[]{:S(2)}) %copy-start.5) | copy-done | bytes 2072
  5.3 0.0 copy-start.6
  5.3 0.7 %copy-done.6 = f32[1,512]{1,0:T(1,128)S(1)} copy-done((f32[1,512]{1,0:T(1,128)S(1)}, f32[1,512]{1,0:T(1,128)}, u32[]{:S(2)}) %copy-start.6) | copy-done | bytes 2072
  5.9 22.2 %shard_map.73 = bf16[512,512]{1,0:T(8,128)(2,1)S(1)} custom-call(bf16[512,512]{1,0:T(8,128)(2,1)S(1)} %copy-done, bf16[512,512]{1,0:T(8,128)(2,1)S(1)} %copy-done.1, bf16[512,512]{1,0:T(8,128)(2,1)S(1)} %copy-done.2, f32[16,32]{1,0:T(8,128)S(1)} %copy-done.4, f32[16,32]{1,0:T(8,128)S(1)} %copy-done.5, f32[3,3,512]{2,1,0:T(4,128)S(1)} %copy-done.3, ...), custom_call_target="tpu_custom_call" | custom-call | tf_op jit(solution)/shard_map/pallas_call | solution.py:312
  28.1 0.8 %copy.9 = bf16[512,512]{1,0:T(8,128)(2,1)} copy(bf16[512,512]{1,0:T(8,128)(2,1)S(1)} %shard_map.73) | data formatting | bytes 1048576
Async XLA Ops:
  0.0 1.0 %copy-start = (bf16[512,512]{1,0:T(8,128)(2,1)S(1)}, bf16[512,512]{1,0:T(8,128)(2,1)}, u32[]{:S(2)}) copy-start(bf16[512,512]{1,0:T(8,128)(2,1)} %query.1) | copy-start | bytes 1572868
  1.0 1.0 %copy-start.1 = (bf16[512,512]{1,0:T(8,128)(2,1)S(1)}, bf16[512,512]{1,0:T(8,128)(2,1)}, u32[]{:S(2)}) copy-start(bf16[512,512]{1,0:T(8,128)(2,1)} %key.1) | copy-start | bytes 1572868
  2.1 1.0 %copy-start.2 = (bf16[512,512]{1,0:T(8,128)(2,1)S(1)}, bf16[512,512]{1,0:T(8,128)(2,1)}, u32[]{:S(2)}) copy-start(bf16[512,512]{1,0:T(8,128)(2,1)} %value.1) | copy-start | bytes 1572868
  3.1 0.7 %copy-start.3 = (f32[3,3,512]{2,1,0:T(4,128)S(1)}, f32[3,3,512]{2,1,0:T(4,128)}, u32[]{:S(2)}) copy-start(f32[3,3,512]{2,1,0:T(4,128)} %short_filter.1) | copy-start | bytes 55300
  3.9 0.7 %copy-start.4 = (f32[16,32]{1,0:T(8,128)S(1)}, f32[16,32]{1,0:T(8,128)}, u32[]{:S(2)}) copy-start(f32[16,32]{1,0:T(8,128)} %residues.1) | copy-start | bytes 6148
  4.6 0.7 %copy-start.5 = (f32[16,32]{1,0:T(8,128)S(1)}, f32[16,32]{1,0:T(8,128)}, u32[]{:S(2)}) copy-start(f32[16,32]{1,0:T(8,128)} %decay_rate.1) | copy-start | bytes 6148
  5.3 0.7 %copy-start.6 = (f32[1,512]{1,0:T(1,128)S(1)}, f32[1,512]{1,0:T(1,128)}, u32[]{:S(2)}) copy-start(f32[1,512]{1,0:T(1,128)} %skip_gain.1) | copy-start | bytes 6148

commit v2 on v1

--- a/solution.py
+++ b/solution.py
@@ -308,11 +308,11 @@
     f32 = jnp.float32
     vmem = lambda *shape, dtype=f32: pltpu.VMEM(shape, dtype)
     dma = pltpu.SemaphoreType.DMA
-    anywhere = pl.BlockSpec(memory_space=pl.ANY)
+    hbm = pl.BlockSpec(memory_space=pltpu.HBM)
     return pl.pallas_call(
         kernel,
         out_shape=jax.ShapeDtypeStruct((rows, width), jnp.bfloat16),
-        in_specs=[anywhere] * 7,
+        in_specs=[hbm] * 7,
         out_specs=pl.BlockSpec(memory_space=pltpu.VMEM),
         scratch_shapes=[
             vmem(3, rows, width, dtype=jnp.bfloat16),
@@ -348,7 +348,12 @@
         compiler_params=pltpu.CompilerParams(
             collective_id=0, has_side_effects=True, vmem_limit_bytes=40 * 2**20
         ),
-    )(query_in, key_in, value_in, residues, decay_rate, short_filter, skip_gain)
+    )(
+        *(
+            pltpu.with_memory_space_constraint(a, pltpu.HBM)
+            for a in (query_in, key_in, value_in, residues, decay_rate, short_filter, skip_gain)
+        )
+    )
 
 
 def solution(mesh):

time: 29.3 us -> 24.3 us (0.83)
  local copies, waits for them, and re-layouts: 6.73 us -> 0.8 us
  Pallas kernels: 22.2 us -> 23.4 us
    unnamed x15 -> x1, local copies, waits for them, and re-layouts: 6.73 us -> 0.8 us
    pallas_call x1, Pallas kernels: 22.2 us -> 23.4 us  [body(): pl.pallas_call(kernel, out_shape=jax.ShapeDtypeStruct((rows, width), jnp....]
where the time goes in v2:
time: 24.3 us; the launch traced here: 24.2 us
  Pallas kernels  23.4 us (96%)
  local copies, waits for them, and re-layouts  0.8 us (3%)
    pallas_call x1, Pallas kernels, body(): pl.pallas_call(kernel, out_shape=jax.ShapeDtypeStruct((rows, width), jnp....  23.4 us
    unnamed x1, local copies, waits for them, and re-layouts  0.8 us

profile of v2, /device:TPU:6, one launch (start us, length us, event | category | flops | bytes accessed | tf_op | source)
XLA Modules:
  0.0 24.2 jit_solution(2858329582647373378)
XLA Ops:
  0.0 23.4 %shard_map.73 = bf16[512,512]{1,0:T(8,128)(2,1)S(1)} custom-call(bf16[512,512]{1,0:T(8,128)(2,1)} %query.1, bf16[512,512]{1,0:T(8,128)(2,1)} %key.1, bf16[512,512]{1,0:T(8,128)(2,1)} %value.1, f32[16,32]{1,0:T(8,128)} %residues.1, f32[16,32]{1,0:T(8,128)} %decay_rate.1, f32[3,3,512]{2,1,0:T(4,128)} %short_filter.1, f32[1,512]{1,0:T(1,128)} %skip_gain.1), custom_call_target="tpu_custom_call" | custom-call | tf_op jit(solution)/shard_map/pallas_call | solution.py:312
  23.4 0.8 %copy.9 = bf16[512,512]{1,0:T(8,128)(2,1)} copy(bf16[512,512]{1,0:T(8,128)(2,1)S(1)} %shard_map.73) | data formatting | bytes 1048576

commit v3 on v2

--- a/solution.py
+++ b/solution.py
@@ -46,8 +46,8 @@
     out,
     raw, wide, params_r, params_d, filt, skip,
     decay, weight, gated, final, base, qs, lead_hi, lead_lo,
-    fresh, lines, edge, rim, delta_own, delta, total, totals, own_sum, far_sum,
-    in_sem, line_send, line_recv, delta_send, delta_recv, total_send, total_recv, rim_send, rim_recv,
+    fresh, lines, edge, rim, ends_own, ends, ends_wide, deltas, delta_own, delta_first, total, totals, own_sum, far_sum,
+    in_sem, line_send, line_recv, ends_send, ends_recv, delta_send, delta_recv, total_send, total_recv, rim_send, rim_recv,
 ):
     rows, width = query.shape
     modes, groups = residues.shape
@@ -59,16 +59,16 @@
     me = lax.axis_index("ctx")
     x, z = me // NZ, lax.rem(me, NZ)
 
-    def line_peer(k):
-        return x * NZ + lax.rem(z + k, NZ)
+    others = [i + jnp.where(i >= z, 1, 0) for i in range(NZ - 1)]
+    inner = x < NX - 1
 
     barrier = pltpu.get_barrier_semaphore()
 
     def here(ctx):
         pl.semaphore_signal(barrier, inc=1, device_id={"ctx": ctx}, device_id_type=MESH)
 
-    for k in range(1, NZ):
-        here(line_peer(k))
+    for t in others:
+        pl.when(inner | (t < z))(functools.partial(here, x * NZ + t))
     for k in range(1, NX):
         pl.when(x >= k)(functools.partial(here, me - k * NZ))
     pl.when((z == 0) & (x > 0))(functools.partial(here, me - 1))
@@ -119,14 +119,16 @@
     def short(taps, now, last, older):
         return taps[0] * now + taps[1] * last + taps[2] * older
 
-    for tile in range(tiles):
+    zero = jnp.zeros((SEGS, LANES), f32)
+
+    def pass_a(tile):
         cols = slice(tile * LANES, (tile + 1) * LANES)
         ktaps, vtaps = taps_of(1, cols), taps_of(2, cols)
         rates = [
             jnp.broadcast_to(jnp.exp(-decay[n : n + 1, cols]), (SEGS, LANES)) for n in range(modes)
         ]
 
-        def advance(j, carry, tile=tile, cols=cols, ktaps=ktaps, vtaps=vtaps, rates=rates):
+        def advance(j, carry):
             k1, k2, v1, v2, states = carry
             k0, v0 = segments(1, j, tile), segments(2, j, tile)
             g = short(ktaps, k0, k1, k2) * short(vtaps, v0, v1, v2)
@@ -134,7 +136,6 @@
             states = tuple(s * a + g for s, a in zip(states, rates))
             return k0, k1, v0, v1, states
 
-        zero = jnp.zeros((SEGS, LANES), f32)
         first = (
             segments(1, -1, tile), segments(1, -2, tile),
             segments(2, -1, tile), segments(2, -2, tile),
@@ -142,25 +143,52 @@
         )
         states = lax.fori_loop(0, steps, advance, first, unroll=4)[4]
         for n in range(modes):
-            final[n, :, cols] = states[n]
             powers = [jnp.exp(-decay[n : n + 1, cols] * (steps * s)) for s in (1, 2, 4)]
-            fresh[n : n + 1, cols] = scan_segments(states[n], powers, row)[SEGS - 1 : SEGS]
+            state = scan_segments(states[n], powers, row)
+            final[n, :, cols] = state
+            fresh[n : n + 1, cols] = state[SEGS - 1 : SEGS]
+
+    pass_a(0)
+    pass_a(1)
 
     large[0].wait()
+    for tile in range(tiles):
+        parts = []
+        for p in (1, 2):
+            parts.append(wide[p, tile, FRONT : FRONT + 2])
+            parts.append(wide[p, tile, FRONT + rows - 2 : FRONT + rows])
+        cols = slice(tile * LANES, (tile + 1) * LANES)
+        ends_own[:, cols] = jnp.concatenate(parts, axis=0).astype(jnp.bfloat16)
+    ends[z] = ends_own[...]
     for p in range(3):
         edge[2 * p : 2 * p + 2] = raw[p, rows - 8 : rows].astype(f32)[6:8]
-    pl.semaphore_wait(
-        barrier, NZ - 1 + NX - 1 - x + jnp.where((z == NZ - 1) & (x < NX - 1), 1, 0)
-    )
+    line_count = jnp.where(inner, NZ - 1, NZ - 1 - z)
+    next_line = jnp.where((z == NZ - 1) & inner, 1, 0)
     last = NX * NZ - 1
+
+    @pl.when(me < last)
+    def _():
+        pl.semaphore_wait(barrier, line_count + NX - 1 - x + next_line)
+
     rim_copy = to_device(edge, rim, rim_send, rim_recv, me + 1)
     pl.when(me < last)(rim_copy.start)
-    line_copies = {
-        k: to_device(fresh, lines.at[z], line_send.at[k], line_recv.at[k], line_peer(k))
-        for k in range(1, NZ)
-    }
-    for k in (4, 3, 5, 2, 6, 1, 7):
-        line_copies[k].start()
+
+    def ends_line(t, source):
+        return to_device(
+            ends_own, ends.at[source], ends_send.at[t], ends_recv.at[source], x * NZ + t
+        )
+
+    for t in others:
+        pl.when(inner | (t > z))(ends_line(t, z).start)
+
+    pass_a(2)
+    pass_a(3)
+
+    line_copies = [
+        to_device(fresh, lines.at[z], line_send.at[t], line_recv.at[z], x * NZ + t) for t in others
+    ]
+    for t, copy in zip(others, line_copies):
+        pl.when(inner | (t > z))(copy.start)
     lines[z] = fresh[...]
 
     lane = lax.broadcasted_iota(jnp.int32, (modes, width), 1)
@@ -186,50 +214,43 @@
     widen(0)
     small[3].wait()
 
-    @pl.when(me == 0)
-    def _():
-        rim[...] = jnp.zeros_like(rim)
-
-    pl.when(me > 0)(rim_copy.wait_recv)
-    for tile in range(tiles):
-        cols = slice(tile * LANES, (tile + 1) * LANES)
-        for p in range(3):
-            wide[p, tile, FRONT - 2 : FRONT] = rim[2 * p : 2 * p + 2, cols]
-
-        def head(p, tile=tile, cols=cols):
-            front = wide[p, tile, FRONT - 2 : FRONT + 2]
-            return sum(filt[p, i : i + 1, cols] * front[2 - i : 4 - i] for i in range(3))
-
-        true_head = head(1) * head(2)
-        for i in range(2):
-            at = slice(i * SEGS, i * SEGS + 1)
-            delta_own[i : i + 1, cols] = true_head[i : i + 1] - gated[at, cols]
-            gated[at, cols] = true_head[i : i + 1]
-    delta_copies = {
-        k: to_device(delta_own, delta.at[z], delta_send.at[k], delta_recv.at[k], line_peer(k))
-        for k in range(1, NZ)
-    }
-    for k in (4, 3, 5, 2, 6, 1, 7):
-        delta_copies[k].start()
-    delta[z] = delta_own[...]
-
-    for tile in range(tiles):
+    def head(p, tile, cols):
+        front = jnp.concatenate([rim[2 * p : 2 * p + 2, cols], wide[p, tile, FRONT : FRONT + 2]], 0)
+        return sum(filt[p, i : i + 1, cols] * front[2 - i : 4 - i] for i in range(3))
+
+    def delta_line(t):
+        return to_device(delta_own, delta_first, delta_send.at[t], delta_recv, x * NZ + t)
+
+    def take_rim():
+        @pl.when(me == 0)
+        def _():
+            rim[...] = jnp.zeros_like(rim)
+
+        pl.when(me > 0)(rim_copy.wait_recv)
+        for tile in range(tiles):
+            cols = slice(tile * LANES, (tile + 1) * LANES)
+            true_head = head(1, tile, cols) * head(2, tile, cols)
+            for i in range(2):
+                at = slice(i * SEGS, i * SEGS + 1)
+                delta_own[i : i + 1, cols] = true_head[i : i + 1] - gated[at, cols]
+
+        @pl.when(z == 0)
+        def _():
+            for t in range(1, NZ):
+                delta_line(t).start()
+            delta_first[...] = delta_own[...]
+
+    def pass_b(tile):
         cols = slice(tile * LANES, (tile + 1) * LANES)
         qtaps = taps_of(0, cols)
         gain = jnp.broadcast_to(skip[0:1, cols], (SEGS, LANES))
-        d0, d1 = delta_own[0:1, cols], delta_own[1:2, cols]
         rates, weights, entering = [], [], []
         for n in range(modes):
-            rate = decay[n : n + 1, cols]
-            powers = [jnp.exp(-rate * (steps * s)) for s in (1, 2, 4)]
-            extra = jnp.exp(-rate * (steps - 1.0)) * d0 + jnp.exp(-rate * (steps - 2.0)) * d1
-            state = final[n, :, cols] + jnp.where(row == 0, extra, 0.0)
-            state = scan_segments(state, powers, row)
-            entering.append(jnp.where(row >= 1, pltpu.roll(state, 1, 0), 0.0))
-            rates.append(jnp.broadcast_to(jnp.exp(-rate), (SEGS, LANES)))
+            entering.append(jnp.where(row >= 1, pltpu.roll(final[n, :, cols], 1, 0), 0.0))
+            rates.append(jnp.broadcast_to(jnp.exp(-decay[n : n + 1, cols]), (SEGS, LANES)))
             weights.append(jnp.broadcast_to(weight[n : n + 1, cols], (SEGS, LANES)))
 
-        def respond(j, carry, tile=tile, cols=cols, qtaps=qtaps, gain=gain, rates=rates, weights=weights):
+        def respond(j, carry):
             q1, q2, states = carry
             q0 = segments(0, j, tile)
             g = gated[pl.ds(pl.multiple_of(j * SEGS, SEGS), SEGS), cols]
@@ -237,29 +258,72 @@
             terms = [s * w for s, w in zip(states, weights)] + [gain * g]
             while len(terms) > 1:
                 terms = [sum(terms[i : i + 2]) for i in range(0, len(terms), 2)]
-            q = short(qtaps, q0, q1, q2)
             at = pl.ds(j, SEGS, stride=steps)
-            base[tile, at] = q * terms[0]
-            qs[tile, at] = q
+            base[tile, at] = terms[0]
+            qs[tile, at] = short(qtaps, q0, q1, q2)
             return q0, q1, states
 
         first = (segments(0, -1, tile), segments(0, -2, tile), tuple(entering))
         lax.fori_loop(0, steps, respond, first, unroll=4)
+
+    pass_b(0)
+    pass_b(1)
+    pl.when(z == 0)(take_rim)
+    pass_b(2)
+    pass_b(3)
+    pl.when(z > 0)(take_rim)
+
+    d0, d1 = delta_own[0:1], delta_own[1:2]
+    inverse = jnp.exp(decay[...])
+    rim_state = inverse * (d0 + inverse * d1)
+    excess = jnp.sum(weight[...] * inverse, axis=0, keepdims=True) * d1
+    for tile in range(tiles):
+        cols = slice(tile * LANES, (tile + 1) * LANES)
+        base[tile, 0:1] += skip[0:1, cols] * d0[:, cols] - excess[:, cols]
+        base[tile, 1:2] += skip[0:1, cols] * d1[:, cols]
+        qs[tile, 0:2] = head(0, tile, cols)
 
     block = jnp.exp(-decay[...] * rows)
     late0 = jnp.exp(-decay[...] * (rows - 1.0))
     late1 = jnp.exp(-decay[...] * (rows - 2.0))
     hop = jnp.exp(-decay[...] * (rows * NZ))
-    for k in range(1, NZ):
-        line_copies[k].wait_recv()
-        delta_copies[k].wait_recv()
+    for t in others:
+        pl.when(inner | (t < z))(ends_line(0, t).wait_recv)
+
+    for t in range(NZ):
+        for tile in range(tiles):
+            part = ends[t, :, tile * LANES : (tile + 1) * LANES]
+            ends_wide[tile, 8 * t : 8 * t + 8] = part.astype(f32)
+    for tile in range(tiles):
+        cols = slice(tile * LANES, (tile + 1) * LANES)
+        olds, news = [], []
+        for p in (1, 2):
+            first, second, before2, before1 = [
+                ends_wide[tile, pl.ds(4 * p - 4 + i, NZ, stride=8)] for i in range(4)
+            ]
+            before1, before2 = pltpu.roll(before1, 1, 0), pltpu.roll(before2, 1, 0)
+            now, last1, last2 = [filt[p, i : i + 1, cols] for i in range(3)]
+            old0, old1 = now * first, now * second + last1 * first
+            olds.append((old0, old1))
+            news.append((old0 + last1 * before1 + last2 * before2, old1 + last2 * before1))
+        for i in range(2):
+            deltas[i, :, cols] = news[0][i] * news[1][i] - olds[0][i] * olds[1][i]
+
+    pl.when(z > 0)(delta_line(0).wait_recv)
+    for t in others:
+
+        @pl.when(inner | (t < z))
+        def _(t=t):
+            to_device(fresh, lines.at[t], line_send.at[t], line_recv.at[t], me).wait_recv()
+
     carried = jnp.zeros((modes, width), f32)
     prefix = carried
     for i in range(NZ):
         prefix = jnp.where(z == i, carried, prefix)
-        carried = carried * block + lines[i] + late0 * delta[i, 0:1] + late1 * delta[i, 1:2]
+        e0, e1 = [deltas[j, i : i + 1] if i else delta_first[j : j + 1] for j in range(2)]
+        carried = carried * block + lines[i] + late0 * e0 + late1 * e1
     total[...] = carried
-    own_sum[...] = prefix
+    own_sum[...] = prefix + rim_state
     total_copies = {
         k: to_device(total, totals.at[x], total_send.at[k], total_recv.at[k], me + k * NZ)
         for k in range(1, NX)
@@ -292,19 +356,28 @@
         for i in range(span // LANES):
             t = u * (span // LANES) + i
             part = add[:, i * LANES : (i + 1) * LANES]
-            out[:, t * LANES : (t + 1) * LANES] = (base[t] + qs[t] * part).astype(jnp.bfloat16)
+            out[:, t * LANES : (t + 1) * LANES] = (qs[t] * (base[t] + part)).astype(jnp.bfloat16)
 
     pl.when(me < last)(rim_copy.wait_send)
-    for k in range(1, NZ):
-        line_copies[k].wait_send()
-        delta_copies[k].wait_send()
+    for t, line_copy in zip(others, line_copies):
+
+        @pl.when(inner | (t > z))
+        def _(t=t, line_copy=line_copy):
+            line_copy.wait_send()
+            ends_line(t, z).wait_send()
+
+    @pl.when(z == 0)
+    def _():
+        for t in range(1, NZ):
+            delta_line(t).wait_send()
+
     for k in range(1, NX):
         pl.when(x + k < NX)(total_copies[k].wait_send)
 
 
 def body(query_in, key_in, value_in, residues, decay_rate, short_filter, skip_gain):
     rows, width = query_in.shape
-    modes = residues.shape[0]
+    modes, tiles = residues.shape[0], width // LANES
     f32 = jnp.float32
     vmem = lambda *shape, dtype=f32: pltpu.VMEM(shape, dtype)
     dma = pltpu.SemaphoreType.DMA
@@ -316,7 +389,7 @@
         out_specs=pl.BlockSpec(memory_space=pltpu.VMEM),
         scratch_shapes=[
             vmem(3, rows, width, dtype=jnp.bfloat16),
-            vmem(3, width // LANES, FRONT + rows, LANES),
+            vmem(3, tiles, FRONT + rows, LANES),
             vmem(*residues.shape),
             vmem(*decay_rate.shape),
             vmem(*short_filter.shape),
@@ -325,16 +398,20 @@
             vmem(modes, width),
             vmem(rows, width),
             vmem(modes, SEGS, width),
-            vmem(width // LANES, rows, LANES),
-            vmem(width // LANES, rows, LANES),
+            vmem(tiles, rows, LANES),
+            vmem(tiles, rows, LANES),
             vmem(rows, width, dtype=jnp.bfloat16),
             vmem(rows, width, dtype=jnp.bfloat16),
             vmem(modes, width),
             vmem(NZ, modes, width),
             vmem(8, width),
             vmem(8, width),
+            vmem(8, width, dtype=jnp.bfloat16),
+            vmem(NZ, 8, width, dtype=jnp.bfloat16),
+            vmem(tiles, NZ * 8, LANES),
+            vmem(2, NZ, width),
             vmem(2, width),
-            vmem(NZ, 2, width),
+            vmem(2, width),
             vmem(modes, width),
             vmem(NX, modes, width),
             vmem(modes, width),
@@ -342,6 +419,7 @@
             dma((7,)),
             dma((NZ,)), dma((NZ,)),
             dma((NZ,)), dma((NZ,)),
+            dma((NZ,)), dma,
             dma((NX,)), dma((NX,)),
             dma, dma,
         ],

time: 24.3 us -> 21.6 us (0.89)
  the two profiles are of different devices: /device:TPU:6 before, /device:TPU:86 now
where the time goes in v3:
time: 21.6 us; the launch traced here: 21.4 us
  Pallas kernels  20.6 us (95%)
  local copies, waits for them, and re-layouts  0.8 us (4%)
    pallas_call x1, Pallas kernels, body(): pl.pallas_call(kernel, out_shape=jax.ShapeDtypeStruct((rows, width), jnp....  20.6 us
    unnamed x1, local copies, waits for them, and re-layouts  0.8 us

profile of v3, /device:TPU:86, one launch (start us, length us, event | category | flops | bytes accessed | tf_op | source)
XLA Modules:
  0.0 21.4 jit_solution(6583544848588546583)
XLA Ops:
  0.0 20.6 %shard_map.73 = bf16[512,512]{1,0:T(8,128)(2,1)S(1)} custom-call(bf16[512,512]{1,0:T(8,128)(2,1)} %query.1, bf16[512,512]{1,0:T(8,128)(2,1)} %key.1, bf16[512,512]{1,0:T(8,128)(2,1)} %value.1, f32[16,32]{1,0:T(8,128)} %residues.1, f32[16,32]{1,0:T(8,128)} %decay_rate.1, f32[3,3,512]{2,1,0:T(4,128)} %short_filter.1, f32[1,512]{1,0:T(1,128)} %skip_gain.1), custom_call_target="tpu_custom_call" | custom-call | tf_op jit(solution)/shard_map/pallas_call | solution.py:385
  20.6 0.8 %copy.9 = bf16[512,512]{1,0:T(8,128)(2,1)} copy(bf16[512,512]{1,0:T(8,128)(2,1)S(1)} %shard_map.73) | data formatting | bytes 1048576

commit v4 on v3

v4 whole, which is shorter than its diff:
```python
import functools

import jax
import jax.numpy as jnp
from jax import lax
from jax.experimental import pallas as pl
from jax.experimental.pallas import tpu as pltpu
from jax.sharding import PartitionSpec as P

MESH = pl.DeviceIdType.MESH
NX, NZ = 4, 8
SEGS = 8
LANES = 128
FRONT = 8
LATE = NZ // 2
RELAY = LATE - 1
HALVES = 2


def to_device(src, dst, send, recv, ctx):
    return pltpu.make_async_remote_copy(
        src_ref=src,
        dst_ref=dst,
        send_sem=send,
        recv_sem=recv,
        device_id={"ctx": ctx},
        device_id_type=MESH,
    )


def one_minus_exp(u):
    series = u * (1 - u / 2 * (1 - u / 3 * (1 - u / 4 * (1 - u / 5 * (1 - u / 6 * (1 - u / 7))))))
    return jnp.where(u < 0.3, series, 1 - jnp.exp(-u))


def scan_segments(value, powers, row):
    for power, step in zip(powers, (1, 2, 4)):
        value = value + power * jnp.where(row >= step, pltpu.roll(value, step, 0), 0.0)
    return value


def split_f32(x):
    high = x.astype(jnp.bfloat16)
    return high, x - high.astype(jnp.float32)


def split(x):
    high, rest = split_f32(x)
    return high, rest.astype(jnp.bfloat16)


def kernel(
    query, key, value, residues, decay_rate, short_filter, skip_gain,
    out,
    raw, wide, params_r, params_d, filt, skip,
    decay, weight, gated, final, base, qs, lead_hi, lead_lo,
    fresh, lines, relayed, edge, rim, ends_own, ends, ends_wide, deltas, delta_own, total, totals, own_sum, far_sum,
    in_sem, line_send, line_recv, ends_send, ends_recv, tail_send, tail_recv, total_send, total_recv, rim_send, rim_recv,
    ready,
):
    rows, width = query.shape
    modes, groups = residues.shape
    size = width // groups
    steps = rows // SEGS
    tiles = width // LANES
    pitch = FRONT + steps
    part = width // HALVES
    f32 = jnp.float32

    me = lax.axis_index("ctx")
    x, z = me // NZ, lax.rem(me, NZ)

    inner = x < NX - 1

    early = z < LATE
    parity = lax.rem(z, 2)
    partner = 1 - 2 * parity

    def takes(half):
        return parity == half

    def sends_to(t):
        ahead = t > z
        if t >= LATE:
            ahead &= z >= RELAY
        return ahead | ((t < z) & inner)

    def hears_from(t):
        heard = (t < z) | ((t > z) & inner)
        return heard & early if t < RELAY else heard

    def sends_half(t, half):
        return sends_to(t) if half == t % 2 else sends_to(t) & (t > z)

    def hears_half(t, half):
        return hears_from(t) & ((t < z) | takes(half))

    barrier = pltpu.get_barrier_semaphore()

    def signal(sem, ctx):
        pl.semaphore_signal(sem, inc=1, device_id={"ctx": ctx}, device_id_type=MESH)

    for t in range(NZ):
        pl.when(hears_from(t))(functools.partial(signal, barrier, x * NZ + t))
    pl.when(early & (x > 0))(functools.partial(signal, barrier, x * NZ - 1))
    for k in range(1, NX):
        pl.when(x + k < NX)(functools.partial(signal, barrier, me + k * NZ))
        pl.when(x + k < NX)(functools.partial(signal, barrier, me + k * NZ + partner))

    small = [
        pltpu.make_async_copy(a, b, in_sem.at[i])
        for i, (a, b) in enumerate(
            ((residues, params_r), (decay_rate, params_d), (short_filter, filt), (skip_gain, skip))
        )
    ]
    large = [
        pltpu.make_async_copy(a, raw.at[p], in_sem.at[4 + p])
        for p, a in enumerate((query, key, value))
    ]
    for copy in (small[1], small[0], small[2], large[1], large[2], large[0], small[3]):
        copy.start()

    lane = lax.broadcasted_iota(jnp.int32, (groups, width), 1)
    group = lax.broadcasted_iota(jnp.int32, (groups, width), 0)
    pick = (lane // size == group).astype(f32).astype(jnp.bfloat16)
    pick = jnp.concatenate([pick] * 3, axis=0)

    def per_channel(values):
        high, rest = split_f32(values)
        middle, rest = split_f32(rest)
        parts = jnp.concatenate([high, middle, rest.astype(jnp.bfloat16)], axis=1)
        return jnp.dot(parts, pick, preferred_element_type=f32)

    small[1].wait()
    decay[...] = per_channel(params_d[...])
    row = lax.broadcasted_iota(jnp.int32, (SEGS, LANES), 0)

    def widen(p):
        for t in range(tiles):
            for i in range(SEGS):
                at = i * pitch + FRONT
                wide[p, t, at : at + steps] = raw[
                    p, i * steps : (i + 1) * steps, t * LANES : (t + 1) * LANES
                ].astype(f32)
                if i:
                    wide[p, t, at - FRONT : at] = wide[p, t, at - pitch + steps - FRONT : at - FRONT]
                else:
                    wide[p, t, 0:FRONT] = jnp.zeros((FRONT, LANES), f32)

    large[1].wait()
    widen(1)
    large[2].wait()
    widen(2)
    small[2].wait()

    def segments(p, offset, tile):
        return wide[p, tile, pl.ds(FRONT + offset, SEGS, stride=pitch)]

    def taps_of(p, cols):
        return [jnp.broadcast_to(filt[p, i : i + 1, cols], (SEGS, LANES)) for i in range(3)]

    def short(taps, now, last, older):
        return taps[0] * now + taps[1] * last + taps[2] * older

    zero = jnp.zeros((SEGS, LANES), f32)

    def pass_a(tile):
        cols = slice(tile * LANES, (tile + 1) * LANES)
        ktaps, vtaps = taps_of(1, cols), taps_of(2, cols)
        rates = [
            jnp.broadcast_to(jnp.exp(-decay[n : n + 1, cols]), (SEGS, LANES)) for n in range(modes)
        ]

        def advance(j, carry):
            k1, k2, v1, v2, states = carry
            k0, v0 = segments(1, j, tile), segments(2, j, tile)
            g = short(ktaps, k0, k1, k2) * short(vtaps, v0, v1, v2)
            gated[pl.ds(pl.multiple_of(j * SEGS, SEGS), SEGS), cols] = g
            states = tuple(s * a + g for s, a in zip(states, rates))
            return k0, k1, v0, v1, states

        first = (
            segments(1, -1, tile), segments(1, -2, tile),
            segments(2, -1, tile), segments(2, -2, tile),
            (zero,) * modes,
        )
        states = lax.fori_loop(0, steps, advance, first, unroll=4)[4]
        for n in range(modes):
            powers = [jnp.exp(-decay[n : n + 1, cols] * (steps * s)) for s in (1, 2, 4)]
            state = scan_segments(states[n], powers, row)
            final[n, :, cols] = state
            half, at = divmod(tile * LANES, part)
            fresh[half, n : n + 1, at : at + LANES] = state[SEGS - 1 : SEGS]

    pass_a(0)
    pass_a(1)

    large[0].wait()
    tail = []
    for tile in range(tiles):
        parts = []
        for p in (1, 2):
            parts.append(wide[p, tile, FRONT : FRONT + 2])
            parts.append(wide[p, tile, SEGS * pitch - 2 : SEGS * pitch])
        half, at = divmod(tile * LANES, part)
        ends_own[half, :, at : at + LANES] = jnp.concatenate(parts, axis=0).astype(jnp.bfloat16)
    ends[z] = ends_own[...]
    for p in range(3):
        tail.append(raw[p, rows - 8 : rows].astype(f32)[6:8])
    edge[...] = jnp.concatenate(tail + [jnp.zeros((2, width), f32)], axis=0).astype(jnp.bfloat16)
    last = NX * NZ - 1
    line_count = sum(jnp.where(sends_to(t), 1, 0) for t in range(NZ))
    ends_line_here = (z == NZ - 1) & inner
    pl.semaphore_wait(barrier, line_count + jnp.where(ends_line_here, LATE, 0) + 2 * x)
    for k in range(1, NX):
        pl.when(x >= k)(functools.partial(signal, ready, me - k * NZ))
        pl.when(x >= k)(functools.partial(signal, ready, me - k * NZ + partner))
    rim_copy = to_device(edge, rim, rim_send, rim_recv, me + 1)

    def tail_line(t):
        return to_device(ends_own, ends.at[NZ], tail_send.at[t], tail_recv, (x + 1) * NZ + t)

    @pl.when(ends_line_here)
    def _():
        for t in range(LATE):
            tail_line(t).start()

    def ends_line(t, source, half):
        return to_device(
            ends_own.at[half], ends.at[source, half],
            ends_send.at[t, half], ends_recv.at[source, half], x * NZ + t,
        )

    sooner, later = range(LATE), range(LATE, NZ)
    for half in range(HALVES):
        for t in sooner:
            pl.when(sends_half(t, half))(ends_line(t, z, half).start)

    def line_copy(t, source, half):
        return to_device(
            fresh.at[half], lines.at[source, half],
            line_send.at[t, half], line_recv.at[source, half], x * NZ + t,
        )

    def send_states(half):
        for t in sooner:
            pl.when(sends_half(t, half))(line_copy(t, z, half).start)
        lines[z, half] = fresh[half]

    send_states(0)
    pass_a(2)
    pass_a(3)
    send_states(1)

    small[0].wait()
    weight[...] = per_channel(params_r[...]) * jnp.sqrt(one_minus_exp(2.0 * decay[...]))

    lane = lax.broadcasted_iota(jnp.int32, (modes, width), 1)
    mode = lax.broadcasted_iota(jnp.int32, (modes, width), 0)
    own = lax.rem(lane, modes) == mode
    flat_rate = jnp.sum(jnp.where(own, decay[...], 0.0), axis=0, keepdims=True)
    flat_weight = jnp.sum(jnp.where(own, weight[...], 0.0), axis=0, keepdims=True)
    for tile in range(tiles):
        cols = slice(tile * LANES, (tile + 1) * LANES)
        rate8 = jnp.broadcast_to(flat_rate[:, cols], (16, LANES))
        row16 = lax.broadcasted_iota(jnp.int32, (16, LANES), 0).astype(f32)
        begin = flat_weight[:, cols] * jnp.exp(-rate8 * (row16 + 1.0))
        jump = jnp.exp(-rate8 * 16.0)

        def lead_rows(i, now, cols=cols, jump=jump):
            at = pl.ds(pl.multiple_of(i * 16, 16), 16)
            hi, lo = split(now)
            lead_hi[at, cols] = hi
            lead_lo[at, cols] = lo
            return now * jump

        lax.fori_loop(0, rows // 16, lead_rows, begin, unroll=4)
    pl.when(me < last)(rim_copy.start)
    for t in later:

        for half in range(HALVES):

            @pl.when(sends_half(t, half) & (z >= LATE))
            def _(t=t, half=half):
                ends_line(t, z, half).start()
                line_copy(t, z, half).start()

    widen(0)
    small[3].wait()

    def head(p, tile, cols):
        before = rim[:, cols].astype(f32)[2 * p : 2 * p + 2]
        front = jnp.concatenate([before, wide[p, tile, FRONT : FRONT + 2]], axis=0)
        return sum(filt[p, i : i + 1, cols] * front[2 - i : 4 - i] for i in range(3))

    def take_rim():
        @pl.when(me == 0)
        def _():
            rim[...] = jnp.zeros_like(rim)

        pl.when(me > 0)(rim_copy.wait_recv)
        for tile in range(tiles):
            cols = slice(tile * LANES, (tile + 1) * LANES)
            true_head = head(1, tile, cols) * head(2, tile, cols)
            for i in range(2):
                at = slice(i * SEGS, i * SEGS + 1)
                delta_own[i : i + 1, cols] = true_head[i : i + 1] - gated[at, cols]

    def pass_b(tile):
        cols = slice(tile * LANES, (tile + 1) * LANES)
        qtaps = taps_of(0, cols)
        gain = jnp.broadcast_to(skip[0:1, cols], (SEGS, LANES))
        rates, weights, entering = [], [], []
        for n in range(modes):
            entering.append(jnp.where(row >= 1, pltpu.roll(final[n, :, cols], 1, 0), 0.0))
            rates.append(jnp.broadcast_to(jnp.exp(-decay[n : n + 1, cols]), (SEGS, LANES)))
            weights.append(jnp.broadcast_to(weight[n : n + 1, cols], (SEGS, LANES)))

        def respond(j, carry):
            q1, q2, states = carry
            q0 = segments(0, j, tile)
            g = gated[pl.ds(pl.multiple_of(j * SEGS, SEGS), SEGS), cols]
            states = tuple(s * a + g for s, a in zip(states, rates))
            terms = [s * w for s, w in zip(states, weights)] + [gain * g]
            while len(terms) > 1:
                terms = [sum(terms[i : i + 2]) for i in range(0, len(terms), 2)]
            at = pl.ds(j, SEGS, stride=steps)
            base[tile, at] = terms[0]
            qs[tile, at] = short(qtaps, q0, q1, q2)
            return q0, q1, states

        first = (segments(0, -1, tile), segments(0, -2, tile), tuple(entering))
        lax.fori_loop(0, steps, respond, first, unroll=4)

    def corrections(known):
        for t in known:
            for tile in range(tiles):
                half, at = divmod(tile * LANES, part)
                piece = ends[t, half, :, at : at + LANES]
                ends_wide[tile, 8 * t : 8 * t + 8] = piece.astype(f32)
        for tile in range(tiles):
            cols = slice(tile * LANES, (tile + 1) * LANES)
            olds, news = [], []
            for p in (1, 2):
                first, second, before2, before1 = [
                    ends_wide[tile, pl.ds(4 * p - 4 + i, NZ, stride=8)] for i in range(4)
                ]
                line_before = jnp.where(x > 0, ends_wide[tile, 8 * NZ + 4 * p - 2 : 8 * NZ + 4 * p], 0.0)
                before2 = jnp.where(row == 0, line_before[0:1], pltpu.roll(before2, 1, 0))
                before1 = jnp.where(row == 0, line_before[1:2], pltpu.roll(before1, 1, 0))
                now, last1, last2 = [filt[p, i : i + 1, cols] for i in range(3)]
                old0, old1 = now * first, now * second + last1 * first
                olds.append((old0, old1))
                news.append((old0 + last1 * before1 + last2 * before2, old1 + last2 * before1))
            for i in range(2):
                deltas[i, :, cols] = news[0][i] * news[1][i] - olds[0][i] * olds[1][i]

    def own_factors(half):
        rate = decay[:, half * part : (half + 1) * part]
        return jnp.exp(-rate * rows), jnp.exp(-rate * (rows - 1.0)), jnp.exp(-rate * (rows - 2.0))

    def add_line(i, half, carried, block, late0, late1):
        cols = slice(half * part, (half + 1) * part)
        e0, e1 = [deltas[j, i : i + 1, cols] for j in range(2)]
        return carried * block + lines[i, half] + late0 * e0 + late1 * e1

    def relay_copy(t, half):
        return to_device(
            relayed.at[half], lines.at[RELAY, half],
            line_send.at[t, half], line_recv.at[RELAY, half], x * NZ + t,
        )

    def relay():
        for half in range(HALVES):
            for t in range(RELAY):
                ends_line(0, t, half).wait_recv()
                line_copy(0, t, half).wait_recv()
        pl.when(x > 0)(tail_line(0).wait_recv)
        corrections([*range(LATE), NZ])
        for half in range(HALVES):
            factors = own_factors(half)
            carried = jnp.zeros((modes, part), f32)
            for i in range(LATE):
                carried = add_line(i, half, carried, *factors)
            relayed[half] = carried
        for t in later:
            for half in range(HALVES):
                ends_line(t, z, half).start()
                relay_copy(t, half).start()

    pass_b(0)
    pass_b(1)
    pass_b(2)
    pl.when(z == RELAY)(relay)
    pass_b(3)

    pl.when((z < RELAY) & (x > 0))(tail_line(0).wait_recv)
    for half in range(HALVES):
        for t in range(NZ):
            heard = hears_half(t, half)
            if t < RELAY:
                heard &= z != RELAY
            pl.when(heard)(ends_line(0, t, half).wait_recv)

    corrections(range(NZ + 1))
    def total_copy(k, source, half, shift=0):
        way = 0 if isinstance(shift, int) else 1
        return to_device(
            total.at[half], totals.at[source, half],
            total_send.at[way, k, half], total_recv.at[source, half], me + k * NZ + shift,
        )

    def sum_line(half, upto=None):
        factors = own_factors(half)
        carried = jnp.zeros((modes, part), f32)
        for i in range(NZ):
            after = add_line(i, half, carried, *factors)
            if i == RELAY:
                after = jnp.where(early, after, lines[RELAY, half])
            carried = after if upto is None else jnp.where(upto > i, after, carried)
        return carried

    for half in range(HALVES):
        for t in range(NZ):
            heard = hears_half(t, half)
            if t < RELAY:
                heard &= z != RELAY
            pl.when(heard)(line_copy(0, t, half).wait_recv)

        @pl.when(takes(half) & inner)
        def _(half=half):
            total[half] = sum_line(half)

    pl.when(inner)(lambda: pl.semaphore_wait(ready, 2 * (NX - 1 - x)))
    for half in range(HALVES):
        for k in range(1, NX):
            pl.when((x + k < NX) & takes(half))(total_copy(k, x, half).start)
            pl.when((x + k < NX) & takes(half))(total_copy(k, x, half, partner).start)

    take_rim()
    d0, d1 = delta_own[0:1], delta_own[1:2]
    inverse = jnp.exp(decay[...])
    rim_state = inverse * (d0 + inverse * d1)
    excess = jnp.sum(weight[...] * inverse, axis=0, keepdims=True) * d1
    for tile in range(tiles):
        cols = slice(tile * LANES, (tile + 1) * LANES)
        base[tile, 0:1] += skip[0:1, cols] * d0[:, cols] - excess[:, cols]
        base[tile, 1:2] += skip[0:1, cols] * d1[:, cols]
        qs[tile, 0:2] = head(0, tile, cols)

    for half in range(HALVES):
        own_sum[half] = sum_line(half, z) + rim_state[:, half * part : (half + 1) * part]

    states = []
    for half in range(HALVES):
        rate = decay[:, half * part : (half + 1) * part]
        hop = jnp.exp(-rate * (rows * NZ))
        into_line = jnp.exp(-rate * (rows * z.astype(f32)))
        far_sum[...] = jnp.zeros_like(far_sum)
        for i in range(NX - 1):

            @pl.when(x > i)
            def _(i=i, half=half, hop=hop):
                total_copy(0, i, half).wait_recv()
                far_sum[...] = far_sum[...] * hop + totals[i, half]

        states.append(own_sum[half] + into_line * far_sum[...])

    grow = lax.broadcasted_iota(jnp.int32, (part, part), 0) // modes
    gcol = lax.broadcasted_iota(jnp.int32, (part, part), 1) // size
    for half in range(HALVES):
        cols = slice(half * part, (half + 1) * part)
        blocks = jnp.concatenate([states[half]] * (part // modes), axis=0)
        hi, lo = split(jnp.where(grow == gcol, blocks, 0.0))
        lh, ll = lead_hi[:, cols], lead_lo[:, cols]
        add = jnp.dot(lh, hi, preferred_element_type=f32)
        add += jnp.dot(lh, lo, preferred_element_type=f32)
        add += jnp.dot(ll, hi, preferred_element_type=f32)
        for t in range(half * part // LANES, (half + 1) * part // LANES):
            more = add[:, t * LANES - half * part : (t + 1) * LANES - half * part]
            out[:, t * LANES : (t + 1) * LANES] = (qs[t] * (base[t] + more)).astype(jnp.bfloat16)

    pl.when(me < last)(rim_copy.wait_send)
    for t in range(NZ):
        for half in range(HALVES):

            @pl.when(sends_half(t, half))
            def _(t=t, half=half):
                ends_line(t, z, half).wait_send()
                line_copy(t, z, half).wait_send()

    @pl.when(ends_line_here)
    def _():
        for t in range(LATE):
            tail_line(t).wait_send()

    for k in range(1, NX):

        @pl.when(x + k < NX)
        def _(k=k):
            for half in range(HALVES):
                pl.when(takes(half))(total_copy(k, x, half).wait_send)
                pl.when(takes(half))(total_copy(k, x, half, partner).wait_send)


def body(query_in, key_in, value_in, residues, decay_rate, short_filter, skip_gain):
    rows, width = query_in.shape
    modes, tiles = residues.shape[0], width // LANES
    pitched = FRONT * SEGS + rows
    half = (modes, width // HALVES)
    f32 = jnp.float32
    vmem = lambda *shape, dtype=f32: pltpu.VMEM(shape, dtype)
    dma = pltpu.SemaphoreType.DMA
    hbm = pl.BlockSpec(memory_space=pltpu.HBM)
    return pl.pallas_call(
        kernel,
        out_shape=jax.ShapeDtypeStruct((rows, width), jnp.bfloat16),
        in_specs=[hbm] * 7,
        out_specs=pl.BlockSpec(memory_space=pltpu.VMEM),
        scratch_shapes=[
            vmem(3, rows, width, dtype=jnp.bfloat16),
            vmem(3, tiles, pitched, LANES),
            vmem(*residues.shape),
            vmem(*decay_rate.shape),
            vmem(*short_filter.shape),
            vmem(*skip_gain.shape),
            vmem(modes, width),
            vmem(modes, width),
            vmem(rows, width),
            vmem(modes, SEGS, width),
            vmem(tiles, rows, LANES),
            vmem(tiles, rows, LANES),
            vmem(rows, width, dtype=jnp.bfloat16),
            vmem(rows, width, dtype=jnp.bfloat16),
            vmem(HALVES, *half),
            vmem(NZ, HALVES, *half),
            vmem(HALVES, *half),
            vmem(8, width, dtype=jnp.bfloat16),
            vmem(8, width, dtype=jnp.bfloat16),
            vmem(HALVES, 8, width // HALVES, dtype=jnp.bfloat16),
            vmem(NZ + 1, HALVES, 8, width // HALVES, dtype=jnp.bfloat16),
            vmem(tiles, NZ * 8 + 8, LANES),
            vmem(2, NZ, width),
            vmem(2, width),
            vmem(HALVES, *half),
            vmem(NX, HALVES, *half),
            vmem(HALVES, *half),
            vmem(*half),
            dma((7,)),
            dma((NZ, HALVES)), dma((NZ, HALVES)),
            dma((NZ, HALVES)), dma((NZ, HALVES)),
            dma((LATE,)), dma,
            dma((2, NX, HALVES)), dma((NX, HALVES)),
            dma, dma,
            pltpu.SemaphoreType.REGULAR,
        ],
        compiler_params=pltpu.CompilerParams(
            collective_id=0, has_side_effects=True, vmem_limit_bytes=40 * 2**20
        ),
    )(
        *(
            pltpu.with_memory_space_constraint(a, pltpu.HBM)
            for a in (query_in, key_in, value_in, residues, decay_rate, short_filter, skip_gain)
        )
    )


def solution(mesh):
    placed = (
        P("ctx", "fsdp"),
        P("ctx", "fsdp"),
        P("ctx", "fsdp"),
        P(None, "fsdp"),
        P(None, "fsdp"),
        P(None, None, "fsdp"),
        P(None, "fsdp"),
    )
    return jax.shard_map(
        body, mesh=mesh, in_specs=placed, out_specs=P("ctx", "fsdp"), check_vma=False
    )
```

time: 21.6 us -> 20.3 us (0.940)
  the two profiles are of different devices: /device:TPU:86 before, /device:TPU:6 now
where the time goes in v4:
time: 20.3 us; the launch traced here: 20.1 us
  Pallas kernels  19.3 us (95%)
  local copies, waits for them, and re-layouts  0.8 us (4%)
    pallas_call x1, Pallas kernels, body(): pl.pallas_call(kernel, out_shape=jax.ShapeDtypeStruct((rows, width), jnp....  19.3 us
    unnamed x1, local copies, waits for them, and re-layouts  0.8 us

profile of v4, /device:TPU:6, one launch (start us, length us, event | category | flops | bytes accessed | tf_op | source)
XLA Modules:
  0.0 20.1 jit_solution(7495436656409328881)
XLA Ops:
  0.0 19.3 %shard_map.73 = bf16[512,512]{1,0:T(8,128)(2,1)S(1)} custom-call(bf16[512,512]{1,0:T(8,128)(2,1)} %query.1, bf16[512,512]{1,0:T(8,128)(2,1)} %key.1, bf16[512,512]{1,0:T(8,128)(2,1)} %value.1, f32[16,32]{1,0:T(8,128)} %residues.1, f32[16,32]{1,0:T(8,128)} %decay_rate.1, f32[3,3,512]{2,1,0:T(4,128)} %short_filter.1, f32[1,512]{1,0:T(1,128)} %skip_gain.1), custom_call_target="tpu_custom_call" | custom-call | tf_op jit(solution)/shard_map/pallas_call | solution.py:515
  19.4 0.8 %copy.9 = bf16[512,512]{1,0:T(8,128)(2,1)} copy(bf16[512,512]{1,0:T(8,128)(2,1)S(1)} %shard_map.73) | data formatting | bytes 1048576

commit v5 on v4

--- a/solution.py
+++ b/solution.py
@@ -28,6 +28,21 @@
     )
 
 
+def wait_for(semaphore, slots, count, most, send=False):
+    for n in [count] if isinstance(count, int) else range(1, most + 1):
+        some = slots.at[pl.ds(0, n)]
+        copy = to_device(some, some, semaphore, semaphore, 0)
+        pl.when(count == n)(copy.wait_send if send else copy.wait_recv)
+
+
+def slot(source, half):
+    return source * HALVES + half
+
+
+def count_of(conditions):
+    return sum(jnp.where(condition, 1, 0) for condition in conditions)
+
+
 def one_minus_exp(u):
     series = u * (1 - u / 2 * (1 - u / 3 * (1 - u / 4 * (1 - u / 5 * (1 - u / 6 * (1 - u / 7))))))
     return jnp.where(u < 0.3, series, 1 - jnp.exp(-u))
@@ -54,8 +69,8 @@
     out,
     raw, wide, params_r, params_d, filt, skip,
     decay, weight, gated, final, base, qs, lead_hi, lead_lo,
-    fresh, lines, relayed, edge, rim, ends_own, ends, ends_wide, deltas, delta_own, total, totals, own_sum, far_sum,
-    in_sem, line_send, line_recv, ends_send, ends_recv, tail_send, tail_recv, total_send, total_recv, rim_send, rim_recv,
+    fresh, lines, relayed, edge, rim, ends_own, ends, ends_wide, deltas, delta_own, total, totals, own_sum,
+    small_sem, large_sem, line_send, line_recv, ends_send, ends_recv, tail_send, tail_recv, total_send, total_recv, rim_send, rim_recv,
     ready,
 ):
     rows, width = query.shape
@@ -67,6 +82,30 @@
     part = width // HALVES
     f32 = jnp.float32
 
+    small = [
+        pltpu.make_async_copy(a, b, small_sem.at[i])
+        for i, (a, b) in enumerate(
+            ((decay_rate, params_d), (short_filter, filt), (residues, params_r), (skip_gain, skip))
+        )
+    ]
+
+    def large(p, half):
+        cols = slice(half * part, (half + 1) * part)
+        source = (query, key, value)[p].at[:, cols]
+        sem = large_sem.at[half if p else HALVES]
+        return pltpu.make_async_copy(source, raw.at[p, :, cols], sem)
+
+    def wait_keys_values(half):
+        both = raw.at[1:3, :, half * part : (half + 1) * part]
+        pltpu.make_async_copy(both, both, large_sem.at[half]).wait()
+
+    small[0].start()
+    large(1, 0).start()
+    large(2, 0).start()
+    small[1].start()
+    large(1, 1).start()
+    large(2, 1).start()
+
     me = lax.axis_index("ctx")
     x, z = me // NZ, lax.rem(me, NZ)
 
@@ -77,7 +116,7 @@
     partner = 1 - 2 * parity
 
     def takes(half):
-        return parity == half
+        return parity != half
 
     def sends_to(t):
         ahead = t > z
@@ -90,7 +129,7 @@
         return heard & early if t < RELAY else heard
 
     def sends_half(t, half):
-        return sends_to(t) if half == t % 2 else sends_to(t) & (t > z)
+        return sends_to(t) if half != t % 2 else sends_to(t) & (t > z)
 
     def hears_half(t, half):
         return hears_from(t) & ((t < z) | takes(half))
@@ -107,18 +146,10 @@
         pl.when(x + k < NX)(functools.partial(signal, barrier, me + k * NZ))
         pl.when(x + k < NX)(functools.partial(signal, barrier, me + k * NZ + partner))
 
-    small = [
-        pltpu.make_async_copy(a, b, in_sem.at[i])
-        for i, (a, b) in enumerate(
-            ((residues, params_r), (decay_rate, params_d), (short_filter, filt), (skip_gain, skip))
-        )
-    ]
-    large = [
-        pltpu.make_async_copy(a, raw.at[p], in_sem.at[4 + p])
-        for p, a in enumerate((query, key, value))
-    ]
-    for copy in (small[1], small[0], small[2], large[1], large[2], large[0], small[3]):
-        copy.start()
+    for half in range(HALVES):
+        large(0, half).start()
+    small[2].start()
+    small[3].start()
 
     lane = lax.broadcasted_iota(jnp.int32, (groups, width), 1)
     group = lax.broadcasted_iota(jnp.int32, (groups, width), 0)
@@ -131,27 +162,20 @@
         parts = jnp.concatenate([high, middle, rest.astype(jnp.bfloat16)], axis=1)
         return jnp.dot(parts, pick, preferred_element_type=f32)
 
-    small[1].wait()
+    small[0].wait()
     decay[...] = per_channel(params_d[...])
     row = lax.broadcasted_iota(jnp.int32, (SEGS, LANES), 0)
 
-    def widen(p):
-        for t in range(tiles):
-            for i in range(SEGS):
-                at = i * pitch + FRONT
-                wide[p, t, at : at + steps] = raw[
-                    p, i * steps : (i + 1) * steps, t * LANES : (t + 1) * LANES
-                ].astype(f32)
-                if i:
-                    wide[p, t, at - FRONT : at] = wide[p, t, at - pitch + steps - FRONT : at - FRONT]
-                else:
-                    wide[p, t, 0:FRONT] = jnp.zeros((FRONT, LANES), f32)
-
-    large[1].wait()
-    widen(1)
-    large[2].wait()
-    widen(2)
-    small[2].wait()
+    def widen(p, t):
+        for i in range(SEGS):
+            at = i * pitch + FRONT
+            wide[p, t, at : at + steps] = raw[
+                p, i * steps : (i + 1) * steps, t * LANES : (t + 1) * LANES
+            ].astype(f32)
+            if i:
+                wide[p, t, at - FRONT : at] = wide[p, t, at - pitch + steps - FRONT : at - FRONT]
+            else:
+                wide[p, t, 0:FRONT] = jnp.zeros((FRONT, LANES), f32)
 
     def segments(p, offset, tile):
         return wide[p, tile, pl.ds(FRONT + offset, SEGS, stride=pitch)]
@@ -165,6 +189,10 @@
     zero = jnp.zeros((SEGS, LANES), f32)
 
     def pass_a(tile):
+        for p in (1, 2):
+            if tile == 0 and p == 1:
+                wait_keys_values(0)
+            widen(p, tile)
         cols = slice(tile * LANES, (tile + 1) * LANES)
         ktaps, vtaps = taps_of(1, cols), taps_of(2, cols)
         rates = [
@@ -184,7 +212,7 @@
             segments(2, -1, tile), segments(2, -2, tile),
             (zero,) * modes,
         )
-        states = lax.fori_loop(0, steps, advance, first, unroll=4)[4]
+        states = lax.fori_loop(0, steps, advance, first, unroll=8)[4]
         for n in range(modes):
             powers = [jnp.exp(-decay[n : n + 1, cols] * (steps * s)) for s in (1, 2, 4)]
             state = scan_segments(states[n], powers, row)
@@ -192,22 +220,18 @@
             half, at = divmod(tile * LANES, part)
             fresh[half, n : n + 1, at : at + LANES] = state[SEGS - 1 : SEGS]
 
+    small[1].wait()
     pass_a(0)
     pass_a(1)
 
-    large[0].wait()
-    tail = []
-    for tile in range(tiles):
-        parts = []
+    wait_keys_values(1)
+    for half in range(HALVES):
+        cols = slice(half * part, (half + 1) * part)
+        ends_rows = []
         for p in (1, 2):
-            parts.append(wide[p, tile, FRONT : FRONT + 2])
-            parts.append(wide[p, tile, SEGS * pitch - 2 : SEGS * pitch])
-        half, at = divmod(tile * LANES, part)
-        ends_own[half, :, at : at + LANES] = jnp.concatenate(parts, axis=0).astype(jnp.bfloat16)
-    ends[z] = ends_own[...]
-    for p in range(3):
-        tail.append(raw[p, rows - 8 : rows].astype(f32)[6:8])
-    edge[...] = jnp.concatenate(tail + [jnp.zeros((2, width), f32)], axis=0).astype(jnp.bfloat16)
+            ends_rows.append(raw[p, 0:8, cols].astype(f32)[0:2])
+            ends_rows.append(raw[p, rows - 8 : rows, cols].astype(f32)[6:8])
+        ends_own[half] = jnp.concatenate(ends_rows, axis=0).astype(jnp.bfloat16)
     last = NX * NZ - 1
     line_count = sum(jnp.where(sends_to(t), 1, 0) for t in range(NZ))
     ends_line_here = (z == NZ - 1) & inner
@@ -218,41 +242,46 @@
     rim_copy = to_device(edge, rim, rim_send, rim_recv, me + 1)
 
     def tail_line(t):
-        return to_device(ends_own, ends.at[NZ], tail_send.at[t], tail_recv, (x + 1) * NZ + t)
+        return to_device(ends_own, ends.at[pl.ds(slot(NZ, 0), HALVES)], tail_send, tail_recv, (x + 1) * NZ + t)
 
     @pl.when(ends_line_here)
     def _():
         for t in range(LATE):
             tail_line(t).start()
 
-    def ends_line(t, source, half):
+    def group_of(t):
+        return jnp.where(z < RELAY, 0, 1) if t == RELAY else 1
+
+    def ends_line(t, half):
         return to_device(
-            ends_own.at[half], ends.at[source, half],
-            ends_send.at[t, half], ends_recv.at[source, half], x * NZ + t,
+            ends_own.at[half], ends.at[slot(z, half)],
+            ends_send, ends_recv.at[group_of(t)], x * NZ + t,
         )
 
     sooner, later = range(LATE), range(LATE, NZ)
     for half in range(HALVES):
         for t in sooner:
-            pl.when(sends_half(t, half))(ends_line(t, z, half).start)
-
-    def line_copy(t, source, half):
+            pl.when(sends_half(t, half))(ends_line(t, half).start)
+
+    def line_copy(t, half):
         return to_device(
-            fresh.at[half], lines.at[source, half],
-            line_send.at[t, half], line_recv.at[source, half], x * NZ + t,
+            fresh.at[half], lines.at[slot(z, half)],
+            line_send, line_recv.at[group_of(t), half], x * NZ + t,
         )
 
     def send_states(half):
         for t in sooner:
-            pl.when(sends_half(t, half))(line_copy(t, z, half).start)
-        lines[z, half] = fresh[half]
+            pl.when(sends_half(t, half))(line_copy(t, half).start)
+        lines[slot(z, half)] = fresh[half]
 
     send_states(0)
     pass_a(2)
     pass_a(3)
     send_states(1)
-
-    small[0].wait()
+    for half in range(HALVES):
+        ends[slot(z, half)] = ends_own[half]
+
+    small[2].wait()
     weight[...] = per_channel(params_r[...]) * jnp.sqrt(one_minus_exp(2.0 * decay[...]))
 
     lane = lax.broadcasted_iota(jnp.int32, (modes, width), 1)
@@ -275,6 +304,12 @@
             return now * jump
 
         lax.fori_loop(0, rows // 16, lead_rows, begin, unroll=4)
+    tail = [jnp.zeros((2, width), f32)]
+    for p in (2, 1, 0):
+        if p == 0:
+            pltpu.make_async_copy(raw.at[0], raw.at[0], large_sem.at[HALVES]).wait()
+        tail.insert(0, raw[p, rows - 8 : rows].astype(f32)[6:8])
+    edge[...] = jnp.concatenate(tail, axis=0).astype(jnp.bfloat16)
     pl.when(me < last)(rim_copy.start)
     for t in later:
 
@@ -282,10 +317,11 @@
 
             @pl.when(sends_half(t, half) & (z >= LATE))
             def _(t=t, half=half):
-                ends_line(t, z, half).start()
-                line_copy(t, z, half).start()
-
-    widen(0)
+                ends_line(t, half).start()
+                line_copy(t, half).start()
+
+    for tile in range(tiles):
+        widen(0, tile)
     small[3].wait()
 
     def head(p, tile, cols):
@@ -336,7 +372,7 @@
         for t in known:
             for tile in range(tiles):
                 half, at = divmod(tile * LANES, part)
-                piece = ends[t, half, :, at : at + LANES]
+                piece = ends[slot(t, half), :, at : at + LANES]
                 ends_wide[tile, 8 * t : 8 * t + 8] = piece.astype(f32)
         for tile in range(tiles):
             cols = slice(tile * LANES, (tile + 1) * LANES)
@@ -362,19 +398,18 @@
     def add_line(i, half, carried, block, late0, late1):
         cols = slice(half * part, (half + 1) * part)
         e0, e1 = [deltas[j, i : i + 1, cols] for j in range(2)]
-        return carried * block + lines[i, half] + late0 * e0 + late1 * e1
+        return carried * block + lines[slot(i, half)] + late0 * e0 + late1 * e1
 
     def relay_copy(t, half):
         return to_device(
-            relayed.at[half], lines.at[RELAY, half],
-            line_send.at[t, half], line_recv.at[RELAY, half], x * NZ + t,
+            relayed.at[half], lines.at[slot(RELAY, half)],
+            line_send, line_recv.at[1, half], x * NZ + t,
         )
 
     def relay():
+        wait_for(ends_recv.at[0], ends, RELAY * HALVES, RELAY * HALVES)
         for half in range(HALVES):
-            for t in range(RELAY):
-                ends_line(0, t, half).wait_recv()
-                line_copy(0, t, half).wait_recv()
+            wait_for(line_recv.at[0, half], lines, RELAY, RELAY)
         pl.when(x > 0)(tail_line(0).wait_recv)
         corrections([*range(LATE), NZ])
         for half in range(HALVES):
@@ -385,7 +420,7 @@
             relayed[half] = carried
         for t in later:
             for half in range(HALVES):
-                ends_line(t, z, half).start()
+                ends_line(t, half).start()
                 relay_copy(t, half).start()
 
     pass_b(0)
@@ -395,19 +430,16 @@
     pass_b(3)
 
     pl.when((z < RELAY) & (x > 0))(tail_line(0).wait_recv)
-    for half in range(HALVES):
-        for t in range(NZ):
-            heard = hears_half(t, half)
-            if t < RELAY:
-                heard &= z != RELAY
-            pl.when(heard)(ends_line(0, t, half).wait_recv)
-
+    def heard(half):
+        known = jnp.where(z == RELAY, RELAY, 0)
+        return count_of(hears_half(t, half) for t in range(NZ)) - known
+
+    wait_for(ends_recv.at[1], ends, heard(0) + heard(1), NZ + 2)
     corrections(range(NZ + 1))
     def total_copy(k, source, half, shift=0):
-        way = 0 if isinstance(shift, int) else 1
         return to_device(
-            total.at[half], totals.at[source, half],
-            total_send.at[way, k, half], total_recv.at[source, half], me + k * NZ + shift,
+            total.at[half], totals.at[slot(source, half)],
+            total_send, total_recv.at[half], me + k * NZ + shift,
         )
 
     def sum_line(half, upto=None):
@@ -416,16 +448,12 @@
         for i in range(NZ):
             after = add_line(i, half, carried, *factors)
             if i == RELAY:
-                after = jnp.where(early, after, lines[RELAY, half])
+                after = jnp.where(early, after, lines[slot(RELAY, half)])
             carried = after if upto is None else jnp.where(upto > i, after, carried)
         return carried
 
     for half in range(HALVES):
-        for t in range(NZ):
-            heard = hears_half(t, half)
-            if t < RELAY:
-                heard &= z != RELAY
-            pl.when(heard)(line_copy(0, t, half).wait_recv)
+        wait_for(line_recv.at[1, half], lines, heard(half), NZ - 1)
 
         @pl.when(takes(half) & inner)
         def _(half=half):
@@ -451,26 +479,24 @@
     for half in range(HALVES):
         own_sum[half] = sum_line(half, z) + rim_state[:, half * part : (half + 1) * part]
 
-    states = []
-    for half in range(HALVES):
-        rate = decay[:, half * part : (half + 1) * part]
-        hop = jnp.exp(-rate * (rows * NZ))
-        into_line = jnp.exp(-rate * (rows * z.astype(f32)))
-        far_sum[...] = jnp.zeros_like(far_sum)
-        for i in range(NX - 1):
-
-            @pl.when(x > i)
-            def _(i=i, half=half, hop=hop):
-                total_copy(0, i, half).wait_recv()
-                far_sum[...] = far_sum[...] * hop + totals[i, half]
-
-        states.append(own_sum[half] + into_line * far_sum[...])
+    pl.when(me < last)(rim_copy.wait_send)
+    sent = count_of(sends_half(t, half) for t in range(NZ) for half in range(HALVES))
+    wait_for(ends_send, ends, sent, NZ + RELAY, send=True)
+    wait_for(line_send, lines, sent, NZ + RELAY, send=True)
+    wait_for(tail_send, ends, jnp.where(ends_line_here, LATE * HALVES, 0), LATE * HALVES, send=True)
 
     grow = lax.broadcasted_iota(jnp.int32, (part, part), 0) // modes
     gcol = lax.broadcasted_iota(jnp.int32, (part, part), 1) // size
-    for half in range(HALVES):
+    for half in reversed(range(HALVES)):
         cols = slice(half * part, (half + 1) * part)
-        blocks = jnp.concatenate([states[half]] * (part // modes), axis=0)
+        hop = jnp.exp(-decay[:, cols] * (rows * NZ))
+        into_line = jnp.exp(-decay[:, cols] * (rows * z.astype(f32)))
+        wait_for(total_recv.at[half], totals, x, NX - 1)
+        far = jnp.zeros((modes, part), f32)
+        for i in range(NX - 1):
+            far = jnp.where(x > i, far * hop + totals[slot(i, half)], far)
+        state = own_sum[half] + into_line * far
+        blocks = jnp.concatenate([state] * (part // modes), axis=0)
         hi, lo = split(jnp.where(grow == gcol, blocks, 0.0))
         lh, ll = lead_hi[:, cols], lead_lo[:, cols]
         add = jnp.dot(lh, hi, preferred_element_type=f32)
@@ -480,27 +506,7 @@
             more = add[:, t * LANES - half * part : (t + 1) * LANES - half * part]
             out[:, t * LANES : (t + 1) * LANES] = (qs[t] * (base[t] + more)).astype(jnp.bfloat16)
 
-    pl.when(me < last)(rim_copy.wait_send)
-    for t in range(NZ):
-        for half in range(HALVES):
-
-            @pl.when(sends_half(t, half))
-            def _(t=t, half=half):
-                ends_line(t, z, half).wait_send()
-                line_copy(t, z, half).wait_send()
-
-    @pl.when(ends_line_here)
-    def _():
-        for t in range(LATE):
-            tail_line(t).wait_send()
-
-    for k in range(1, NX):
-
-        @pl.when(x + k < NX)
-        def _(k=k):
-            for half in range(HALVES):
-                pl.when(takes(half))(total_copy(k, x, half).wait_send)
-                pl.when(takes(half))(total_copy(k, x, half, partner).wait_send)
+    wait_for(total_send, totals, 2 * (NX - 1 - x), 2 * (NX - 1), send=True)
 
 
 def body(query_in, key_in, value_in, residues, decay_rate, short_filter, skip_gain):
@@ -533,24 +539,23 @@
             vmem(rows, width, dtype=jnp.bfloat16),
             vmem(rows, width, dtype=jnp.bfloat16),
             vmem(HALVES, *half),
-            vmem(NZ, HALVES, *half),
+            vmem(NZ * HALVES, *half),
             vmem(HALVES, *half),
             vmem(8, width, dtype=jnp.bfloat16),
             vmem(8, width, dtype=jnp.bfloat16),
             vmem(HALVES, 8, width // HALVES, dtype=jnp.bfloat16),
-            vmem(NZ + 1, HALVES, 8, width // HALVES, dtype=jnp.bfloat16),
+            vmem((NZ + 1) * HALVES, 8, width // HALVES, dtype=jnp.bfloat16),
             vmem(tiles, NZ * 8 + 8, LANES),
             vmem(2, NZ, width),
             vmem(2, width),
             vmem(HALVES, *half),
-            vmem(NX, HALVES, *half),
+            vmem(NX * HALVES, *half),
             vmem(HALVES, *half),
-            vmem(*half),
-            dma((7,)),
-            dma((NZ, HALVES)), dma((NZ, HALVES)),
-            dma((NZ, HALVES)), dma((NZ, HALVES)),
-            dma((LATE,)), dma,
-            dma((2, NX, HALVES)), dma((NX, HALVES)),
+            dma((4,)), dma((HALVES + 1,)),
+            dma, dma((2, HALVES)),
+            dma, dma((2,)),
+            dma, dma,
+            dma, dma((HALVES,)),
             dma, dma,
             pltpu.SemaphoreType.REGULAR,
         ],

time: 20.3 us -> 19.9 us (0.980)
  the two profiles are of different devices: /device:TPU:6 before, /device:TPU:230 now
where the time goes in v5:
time: 19.9 us; the launch traced here: 19.8 us
  Pallas kernels  19 us (95%)
  local copies, waits for them, and re-layouts  0.8 us (4%)
    pallas_call x1, Pallas kernels, body(): pl.pallas_call(kernel, out_shape=jax.ShapeDtypeStruct((rows, width), jnp....  19 us
    unnamed x1, local copies, waits for them, and re-layouts  0.8 us

profile of v5, /device:TPU:230, one launch (start us, length us, event | category | flops | bytes accessed | tf_op | source)
XLA Modules:
  0.0 19.8 jit_solution(1732364517786586209)
XLA Ops:
  0.0 19.0 %shard_map.73 = bf16[512,512]{1,0:T(8,128)(2,1)S(1)} custom-call(bf16[512,512]{1,0:T(8,128)(2,1)} %query.1, bf16[512,512]{1,0:T(8,128)(2,1)} %key.1, bf16[512,512]{1,0:T(8,128)(2,1)} %value.1, f32[16,32]{1,0:T(8,128)} %residues.1, f32[16,32]{1,0:T(8,128)} %decay_rate.1, f32[3,3,512]{2,1,0:T(4,128)} %short_filter.1, f32[1,512]{1,0:T(1,128)} %skip_gain.1), custom_call_target="tpu_custom_call" | custom-call | tf_op jit(solution)/shard_map/pallas_call | solution.py:521
  19.0 0.8 %copy.9 = bf16[512,512]{1,0:T(8,128)(2,1)} copy(bf16[512,512]{1,0:T(8,128)(2,1)S(1)} %shard_map.73) | data formatting | bytes 1048576

commit v6 on v5

--- a/solution.py
+++ b/solution.py
@@ -418,15 +418,15 @@
             for i in range(LATE):
                 carried = add_line(i, half, carried, *factors)
             relayed[half] = carried
-        for t in later:
+        for t in reversed(later):
             for half in range(HALVES):
                 ends_line(t, half).start()
                 relay_copy(t, half).start()
 
     pass_b(0)
     pass_b(1)
+    pl.when(z == RELAY)(relay)
     pass_b(2)
-    pl.when(z == RELAY)(relay)
     pass_b(3)
 
     pl.when((z < RELAY) & (x > 0))(tail_line(0).wait_recv)
@@ -462,8 +462,8 @@
     pl.when(inner)(lambda: pl.semaphore_wait(ready, 2 * (NX - 1 - x)))
     for half in range(HALVES):
         for k in range(1, NX):
-            pl.when((x + k < NX) & takes(half))(total_copy(k, x, half).start)
-            pl.when((x + k < NX) & takes(half))(total_copy(k, x, half, partner).start)
+            pl.when((x + k < NX) & takes(half))(total_copy(k, x, half, -parity).start)
+            pl.when((x + k < NX) & takes(half))(total_copy(k, x, half, 1 - parity).start)
 
     take_rim()
     d0, d1 = delta_own[0:1], delta_own[1:2]

time: 19.9 us -> 18.6 us (0.935)
  the two profiles are of different devices: /device:TPU:230 before, /device:TPU:6 now
where the time goes in v6:
time: 18.6 us; the launch traced here: 18.5 us
  Pallas kernels  17.7 us (95%)
  local copies, waits for them, and re-layouts  0.8 us (4%)
    pallas_call x1, Pallas kernels, body(): pl.pallas_call(kernel, out_shape=jax.ShapeDtypeStruct((rows, width), jnp....  17.7 us
    unnamed x1, local copies, waits for them, and re-layouts  0.8 us

profile of v6, /device:TPU:6, one launch (start us, length us, event | category | flops | bytes accessed | tf_op | source)
XLA Modules:
  0.0 18.5 jit_solution(15165063868135637772)
XLA Ops:
  0.0 17.7 %shard_map.73 = bf16[512,512]{1,0:T(8,128)(2,1)S(1)} custom-call(bf16[512,512]{1,0:T(8,128)(2,1)} %query.1, bf16[512,512]{1,0:T(8,128)(2,1)} %key.1, bf16[512,512]{1,0:T(8,128)(2,1)} %value.1, f32[16,32]{1,0:T(8,128)} %residues.1, f32[16,32]{1,0:T(8,128)} %decay_rate.1, f32[3,3,512]{2,1,0:T(4,128)} %short_filter.1, f32[1,512]{1,0:T(1,128)} %skip_gain.1), custom_call_target="tpu_custom_call" | custom-call | tf_op jit(solution)/shard_map/pallas_call | solution.py:521
  17.7 0.8 %copy.9 = bf16[512,512]{1,0:T(8,128)(2,1)} copy(bf16[512,512]{1,0:T(8,128)(2,1)S(1)} %shard_map.73) | data formatting | bytes 1048576

commit v7 on v6

--- a/solution.py
+++ b/solution.py
@@ -166,16 +166,16 @@
     decay[...] = per_channel(params_d[...])
     row = lax.broadcasted_iota(jnp.int32, (SEGS, LANES), 0)
 
+    def widen_segment(p, t, i):
+        cols = slice(t * LANES, (t + 1) * LANES)
+        at = pl.multiple_of(i * pitch, FRONT)
+        now = raw[p, pl.ds(pl.multiple_of(i * steps, steps), steps), cols].astype(f32)
+        wide[p, t, pl.ds(at + FRONT, steps)] = now
+        wide[p, t, pl.ds(at + pitch, FRONT)] = now[steps - FRONT :]
+
     def widen(p, t):
         for i in range(SEGS):
-            at = i * pitch + FRONT
-            wide[p, t, at : at + steps] = raw[
-                p, i * steps : (i + 1) * steps, t * LANES : (t + 1) * LANES
-            ].astype(f32)
-            if i:
-                wide[p, t, at - FRONT : at] = wide[p, t, at - pitch + steps - FRONT : at - FRONT]
-            else:
-                wide[p, t, 0:FRONT] = jnp.zeros((FRONT, LANES), f32)
+            widen_segment(p, t, i)
 
     def segments(p, offset, tile):
         return wide[p, tile, pl.ds(FRONT + offset, SEGS, stride=pitch)]
@@ -189,30 +189,38 @@
     zero = jnp.zeros((SEGS, LANES), f32)
 
     def pass_a(tile):
-        for p in (1, 2):
-            if tile == 0 and p == 1:
-                wait_keys_values(0)
-            widen(p, tile)
+        if tile == 0:
+            wait_keys_values(0)
+        ahead = tile + 1 < tiles
+        if tile == 0:
+            widen(1, 0)
+            widen(2, 0)
         cols = slice(tile * LANES, (tile + 1) * LANES)
         ktaps, vtaps = taps_of(1, cols), taps_of(2, cols)
         rates = [
             jnp.broadcast_to(jnp.exp(-decay[n : n + 1, cols]), (SEGS, LANES)) for n in range(modes)
         ]
 
-        def advance(j, carry):
+        def advance(i, carry):
             k1, k2, v1, v2, states = carry
-            k0, v0 = segments(1, j, tile), segments(2, j, tile)
-            g = short(ktaps, k0, k1, k2) * short(vtaps, v0, v1, v2)
-            gated[pl.ds(pl.multiple_of(j * SEGS, SEGS), SEGS), cols] = g
-            states = tuple(s * a + g for s, a in zip(states, rates))
-            return k0, k1, v0, v1, states
+            for step in range(SEGS):
+                j = i * SEGS + step
+                k0, v0 = segments(1, j, tile), segments(2, j, tile)
+                g = short(ktaps, k0, k1, k2) * short(vtaps, v0, v1, v2)
+                gated[pl.ds(pl.multiple_of(j * SEGS, SEGS), SEGS), cols] = g
+                states = tuple(s * a + g for s, a in zip(states, rates))
+                k1, k2, v1, v2 = k0, k1, v0, v1
+            if ahead:
+                widen_segment(1, tile + 1, i)
+                widen_segment(2, tile + 1, i)
+            return k1, k2, v1, v2, states
 
         first = (
             segments(1, -1, tile), segments(1, -2, tile),
             segments(2, -1, tile), segments(2, -2, tile),
             (zero,) * modes,
         )
-        states = lax.fori_loop(0, steps, advance, first, unroll=8)[4]
+        states = lax.fori_loop(0, steps // SEGS, advance, first)[4]
         for n in range(modes):
             powers = [jnp.exp(-decay[n : n + 1, cols] * (steps * s)) for s in (1, 2, 4)]
             state = scan_segments(states[n], powers, row)
@@ -220,11 +228,14 @@
             half, at = divmod(tile * LANES, part)
             fresh[half, n : n + 1, at : at + LANES] = state[SEGS - 1 : SEGS]
 
+    for p in range(3):
+        for t in range(tiles):
+            wide[p, t, 0:FRONT] = jnp.zeros((FRONT, LANES), f32)
     small[1].wait()
     pass_a(0)
+    wait_keys_values(1)
     pass_a(1)
 
-    wait_keys_values(1)
     for half in range(HALVES):
         cols = slice(half * part, (half + 1) * part)
         ends_rows = []
@@ -236,9 +247,6 @@
     line_count = sum(jnp.where(sends_to(t), 1, 0) for t in range(NZ))
     ends_line_here = (z == NZ - 1) & inner
     pl.semaphore_wait(barrier, line_count + jnp.where(ends_line_here, LATE, 0) + 2 * x)
-    for k in range(1, NX):
-        pl.when(x >= k)(functools.partial(signal, ready, me - k * NZ))
-        pl.when(x >= k)(functools.partial(signal, ready, me - k * NZ + partner))
     rim_copy = to_device(edge, rim, rim_send, rim_recv, me + 1)
 
     def tail_line(t):
@@ -278,6 +286,9 @@
     pass_a(2)
     pass_a(3)
     send_states(1)
+    for k in range(1, NX):
+        pl.when(x >= k)(functools.partial(signal, ready, me - k * NZ))
+        pl.when(x >= k)(functools.partial(signal, ready, me - k * NZ + partner))
     for half in range(HALVES):
         ends[slot(z, half)] = ends_own[half]
 
@@ -460,7 +471,7 @@
             total[half] = sum_line(half)
 
     pl.when(inner)(lambda: pl.semaphore_wait(ready, 2 * (NX - 1 - x)))
-    for half in range(HALVES):
+    for half in reversed(range(HALVES)):
         for k in range(1, NX):
             pl.when((x + k < NX) & takes(half))(total_copy(k, x, half, -parity).start)
             pl.when((x + k < NX) & takes(half))(total_copy(k, x, half, 1 - parity).start)
@@ -498,13 +509,17 @@
         state = own_sum[half] + into_line * far
         blocks = jnp.concatenate([state] * (part // modes), axis=0)
         hi, lo = split(jnp.where(grow == gcol, blocks, 0.0))
-        lh, ll = lead_hi[:, cols], lead_lo[:, cols]
-        add = jnp.dot(lh, hi, preferred_element_type=f32)
-        add += jnp.dot(lh, lo, preferred_element_type=f32)
-        add += jnp.dot(ll, hi, preferred_element_type=f32)
-        for t in range(half * part // LANES, (half + 1) * part // LANES):
-            more = add[:, t * LANES - half * part : (t + 1) * LANES - half * part]
-            out[:, t * LANES : (t + 1) * LANES] = (qs[t] * (base[t] + more)).astype(jnp.bfloat16)
+        for piece in range(2):
+            at = slice(piece * rows // 2, (piece + 1) * rows // 2)
+            lh, ll = lead_hi[at, cols], lead_lo[at, cols]
+            add = jnp.dot(lh, hi, preferred_element_type=f32)
+            add += jnp.dot(lh, lo, preferred_element_type=f32)
+            add += jnp.dot(ll, hi, preferred_element_type=f32)
+            for t in range(half * part // LANES, (half + 1) * part // LANES):
+                more = add[:, t * LANES - half * part : (t + 1) * LANES - half * part]
+                out[at, t * LANES : (t + 1) * LANES] = (
+                    qs[t, at] * (base[t, at] + more)
+                ).astype(jnp.bfloat16)
 
     wait_for(total_send, totals, 2 * (NX - 1 - x), 2 * (NX - 1), send=True)
 
@@ -525,7 +540,7 @@
         out_specs=pl.BlockSpec(memory_space=pltpu.VMEM),
         scratch_shapes=[
             vmem(3, rows, width, dtype=jnp.bfloat16),
-            vmem(3, tiles, pitched, LANES),
+            vmem(3, tiles, pitched + FRONT, LANES),
             vmem(*residues.shape),
             vmem(*decay_rate.shape),
             vmem(*short_filter.shape),

time: 18.6 us -> 18.3 us (0.984)
  Pallas kernels: 17.7 us -> 17.4 us
    pallas_call x1, Pallas kernels: 17.7 us -> 17.4 us  [body(): pl.pallas_call(kernel, out_shape=jax.ShapeDtypeStruct((rows, width), jnp....]
where the time goes in v7:
time: 18.3 us; the launch traced here: 18.2 us
  Pallas kernels  17.4 us (95%)
  local copies, waits for them, and re-layouts  0.8 us (4%)
    pallas_call x1, Pallas kernels, body(): pl.pallas_call(kernel, out_shape=jax.ShapeDtypeStruct((rows, width), jnp....  17.4 us
    unnamed x1, local copies, waits for them, and re-layouts  0.8 us

profile of v7, /device:TPU:6, one launch (start us, length us, event | category | flops | bytes accessed | tf_op | source)
XLA Modules:
  0.0 18.2 jit_solution(7798668697980421165)
XLA Ops:
  0.0 17.4 %shard_map.73 = bf16[512,512]{1,0:T(8,128)(2,1)S(1)} custom-call(bf16[512,512]{1,0:T(8,128)(2,1)} %query.1, bf16[512,512]{1,0:T(8,128)(2,1)} %key.1, bf16[512,512]{1,0:T(8,128)(2,1)} %value.1, f32[16,32]{1,0:T(8,128)} %residues.1, f32[16,32]{1,0:T(8,128)} %decay_rate.1, f32[3,3,512]{2,1,0:T(4,128)} %short_filter.1, f32[1,512]{1,0:T(1,128)} %skip_gain.1), custom_call_target="tpu_custom_call" | custom-call | tf_op jit(solution)/shard_map/pallas_call | solution.py:536
  17.4 0.8 %copy.9 = bf16[512,512]{1,0:T(8,128)(2,1)} copy(bf16[512,512]{1,0:T(8,128)(2,1)S(1)} %shard_map.73) | data formatting | bytes 1048576

commit v8 on v7

--- a/solution.py
+++ b/solution.py
@@ -100,9 +100,9 @@
         pltpu.make_async_copy(both, both, large_sem.at[half]).wait()
 
     small[0].start()
+    small[1].start()
     large(1, 0).start()
     large(2, 0).start()
-    small[1].start()
     large(1, 1).start()
     large(2, 1).start()
 
@@ -236,6 +236,38 @@
     wait_keys_values(1)
     pass_a(1)
 
+    last = NX * NZ - 1
+    line_count = sum(jnp.where(sends_to(t), 1, 0) for t in range(NZ))
+    ends_line_here = (z == NZ - 1) & inner
+    pl.semaphore_wait(barrier, line_count + jnp.where(ends_line_here, LATE, 0) + 2 * x)
+    rim_copy = to_device(edge, rim, rim_send, rim_recv, me + 1)
+
+    def tail_line(t):
+        return to_device(ends_own, ends.at[pl.ds(slot(NZ, 0), HALVES)], tail_send, tail_recv, (x + 1) * NZ + t)
+
+    def group_of(t):
+        return jnp.where(z < RELAY, 0, 1) if t == RELAY else 1
+
+    def ends_line(t, half):
+        return to_device(
+            ends_own.at[half], ends.at[slot(z, half)],
+            ends_send, ends_recv.at[group_of(t)], x * NZ + t,
+        )
+
+    sooner, later = range(LATE), range(LATE, NZ)
+    def line_copy(t, half):
+        return to_device(
+            fresh.at[half], lines.at[slot(z, half)],
+            line_send, line_recv.at[group_of(t), half], x * NZ + t,
+        )
+
+    def send_states(half):
+        for t in sooner:
+            pl.when(sends_half(t, half))(line_copy(t, half).start)
+        lines[slot(z, half)] = fresh[half]
+
+    send_states(0)
+
     for half in range(HALVES):
         cols = slice(half * part, (half + 1) * part)
         ends_rows = []
@@ -243,46 +275,16 @@
             ends_rows.append(raw[p, 0:8, cols].astype(f32)[0:2])
             ends_rows.append(raw[p, rows - 8 : rows, cols].astype(f32)[6:8])
         ends_own[half] = jnp.concatenate(ends_rows, axis=0).astype(jnp.bfloat16)
-    last = NX * NZ - 1
-    line_count = sum(jnp.where(sends_to(t), 1, 0) for t in range(NZ))
-    ends_line_here = (z == NZ - 1) & inner
-    pl.semaphore_wait(barrier, line_count + jnp.where(ends_line_here, LATE, 0) + 2 * x)
-    rim_copy = to_device(edge, rim, rim_send, rim_recv, me + 1)
-
-    def tail_line(t):
-        return to_device(ends_own, ends.at[pl.ds(slot(NZ, 0), HALVES)], tail_send, tail_recv, (x + 1) * NZ + t)
 
     @pl.when(ends_line_here)
     def _():
         for t in range(LATE):
             tail_line(t).start()
 
-    def group_of(t):
-        return jnp.where(z < RELAY, 0, 1) if t == RELAY else 1
-
-    def ends_line(t, half):
-        return to_device(
-            ends_own.at[half], ends.at[slot(z, half)],
-            ends_send, ends_recv.at[group_of(t)], x * NZ + t,
-        )
-
-    sooner, later = range(LATE), range(LATE, NZ)
     for half in range(HALVES):
         for t in sooner:
             pl.when(sends_half(t, half))(ends_line(t, half).start)
 
-    def line_copy(t, half):
-        return to_device(
-            fresh.at[half], lines.at[slot(z, half)],
-            line_send, line_recv.at[group_of(t), half], x * NZ + t,
-        )
-
-    def send_states(half):
-        for t in sooner:
-            pl.when(sends_half(t, half))(line_copy(t, half).start)
-        lines[slot(z, half)] = fresh[half]
-
-    send_states(0)
     pass_a(2)
     pass_a(3)
     send_states(1)
@@ -453,8 +455,15 @@
             total_send, total_recv.at[half], me + k * NZ + shift,
         )
 
+    all_factors = [own_factors(half) for half in range(HALVES)]
+    hops, into_lines = [], []
+    for half in range(HALVES):
+        rate = decay[:, half * part : (half + 1) * part]
+        hops.append(jnp.exp(-rate * (rows * NZ)))
+        into_lines.append(jnp.exp(-rate * (rows * z.astype(f32))))
+
     def sum_line(half, upto=None):
-        factors = own_factors(half)
+        factors = all_factors[half]
         carried = jnp.zeros((modes, part), f32)
         for i in range(NZ):
             after = add_line(i, half, carried, *factors)
@@ -500,8 +509,7 @@
     gcol = lax.broadcasted_iota(jnp.int32, (part, part), 1) // size
     for half in reversed(range(HALVES)):
         cols = slice(half * part, (half + 1) * part)
-        hop = jnp.exp(-decay[:, cols] * (rows * NZ))
-        into_line = jnp.exp(-decay[:, cols] * (rows * z.astype(f32)))
+        hop, into_line = hops[half], into_lines[half]
         wait_for(total_recv.at[half], totals, x, NX - 1)
         far = jnp.zeros((modes, part), f32)
         for i in range(NX - 1):

time: 18.3 us -> 18.4 us (level)
  no operation moved by 1% of the time
where the time goes in v8:
time: 18.4 us; the launch traced here: 18.3 us
  Pallas kernels  17.5 us (95%)
  local copies, waits for them, and re-layouts  0.8 us (4%)
    pallas_call x1, Pallas kernels, body(): pl.pallas_call(kernel, out_shape=jax.ShapeDtypeStruct((rows, width), jnp....  17.5 us
    unnamed x1, local copies, waits for them, and re-layouts  0.8 us

profile of v8, /device:TPU:6, one launch (start us, length us, event | category | flops | bytes accessed | tf_op | source)
XLA Modules:
  0.0 18.3 jit_solution(16370095653468246489)
XLA Ops:
  0.0 17.5 %shard_map.73 = bf16[512,512]{1,0:T(8,128)(2,1)S(1)} custom-call(bf16[512,512]{1,0:T(8,128)(2,1)} %query.1, bf16[512,512]{1,0:T(8,128)(2,1)} %key.1, bf16[512,512]{1,0:T(8,128)(2,1)} %value.1, f32[16,32]{1,0:T(8,128)} %residues.1, f32[16,32]{1,0:T(8,128)} %decay_rate.1, f32[3,3,512]{2,1,0:T(4,128)} %short_filter.1, f32[1,512]{1,0:T(1,128)} %skip_gain.1), custom_call_target="tpu_custom_call" | custom-call | tf_op jit(solution)/shard_map/pallas_call | solution.py:544
  17.5 0.8 %copy.9 = bf16[512,512]{1,0:T(8,128)(2,1)} copy(bf16[512,512]{1,0:T(8,128)(2,1)S(1)} %shard_map.73) | data formatting | bytes 1048576
